TPU v7x, 512 devices: a whole 4x4x16 slice. The times are simulated.
512 devices in a mesh: grp: 8 (over x, core), path: 64 (over z, y).
Axes of the slice: x: 4, y: 4, z: 16, core: 2. Of those that a mesh axis runs over, the one named last changes fastest.
Arguments:
- normals: float32 [32, 8388608], P(None, ('grp', 'path')), may hold values from -10.1 to 10.1
- spot_today: float32 [32], replicated, may hold values from 0.5 to 2
- volatility: float32 [32], replicated, may hold values from 0.1 to 0.5
- weights: float32 [32], replicated, may hold values from 0.5 to 1.5
- cash_flows: float32 [8388608], P(('grp', 'path')), may hold values from -300 to 300
- exercise: int32 [8388608], P(('grp', 'path')), may hold values 0 or 1
Outputs:
- path_value: float32 [8388608], P(('grp', 'path'))
- state_cot: float32 [32, 8388608], P(None, ('grp', 'path'))
- flow_cot: float32 [8388608], P(('grp', 'path'))
- greeks: float32 [2, 32], replicated
All inputs are finite; a program needn't handle non-finite values. No bound on the sum of `exercise` on one device may be relied on, other than what follows from the above.
Results may differ from a plain program's by a relative error of at most 0.0003.
Values sent between devices are 32-bit elements; how exact they have to be, the bound alone decides.
A program may use at most 64 MiB of HBM per device.

v0:
```python
import math

import jax
import jax.numpy as jnp
from jax import lax
from jax.sharding import PartitionSpec as P

expiry_time = 0.5
root_time = math.sqrt(0.5)
inv_root_two = 1.0 / math.sqrt(2.0)
notional = 20.0
soft_width = 0.02


def path_state(normals, spot_today, volatility):
    return spot_today[:, None] * jnp.exp(
        volatility[:, None] * (root_time * normals) - 0.5 * expiry_time * volatility[:, None] ** 2
    )


def basis_rows(state, spot_today, volatility):
    scaled = (state / spot_today[:, None] - 1.0) / (volatility[:, None] * root_time)
    leading = jnp.ones_like(scaled[:1])
    squares = (scaled * scaled - 1.0) * inv_root_two
    neighbour = scaled * jnp.roll(scaled, -1, axis=0)
    bounded = jnp.tanh(scaled[:-1])
    return jnp.concatenate([leading, scaled, squares, neighbour, bounded], axis=0)


def payoff(state, spot_today, weights):
    basket = jnp.sum(weights[:, None] * state, axis=0) / jnp.sum(weights * spot_today)
    return notional * soft_width * jax.nn.softplus((basket - 1.0) / soft_width)


def chol_solve(factor, rhs):
    first = lax.linalg.triangular_solve(factor, rhs, left_side=True, lower=True)
    return lax.linalg.triangular_solve(factor, first, left_side=True, lower=True, transpose_a=True)


def per_device(normals, spot_today, volatility, weights, cash_flows, exercise):
    assets, local_paths = normals.shape
    features = 4 * assets
    block_width = math.gcd(local_paths, 1024)
    block_count = local_paths // block_width
    path_total = local_paths * lax.axis_size("grp") * lax.axis_size("path")
    highest = lax.Precision.HIGHEST
    contract_last = (((1,), (1,)), ((), ()))

    def block_inputs(block_index):
        block_start = block_index * block_width
        draw_block = lax.dynamic_slice_in_dim(normals, block_start, block_width, 1)
        flow_block = lax.dynamic_slice_in_dim(cash_flows, block_start, block_width, 0)
        taken_flag = lax.dynamic_slice_in_dim(exercise, block_start, block_width, 0).astype(
            jnp.float32
        )
        return (draw_block, flow_block, taken_flag)

    def gram_step(block_index, running):
        gram_acc, moment_acc = running
        draw_block, flow_block, taken_flag = block_inputs(block_index)
        basis_block = basis_rows(
            path_state(draw_block, spot_today, volatility), spot_today, volatility
        )
        gram_acc = gram_acc + lax.dot_general(
            basis_block,
            basis_block,
            contract_last,
            precision=highest,
            preferred_element_type=jnp.float32,
        )
        targets = jnp.stack([flow_block, 1.0 - taken_flag])
        moment_acc = moment_acc + lax.dot_general(
            targets,
            basis_block,
            contract_last,
            precision=highest,
            preferred_element_type=jnp.float32,
        )
        return (gram_acc, moment_acc)

    zero_gram = jnp.zeros((features, features), jnp.float32)
    zero_moment = jnp.zeros((2, features), jnp.float32)
    gram_acc, moment_acc = lax.fori_loop(0, block_count, gram_step, (zero_gram, zero_moment))
    gram_sum, moment_sum = lax.psum((gram_acc, moment_acc), ("grp", "path"))
    gram_mean = gram_sum / path_total
    moment_mean = moment_sum / path_total
    factor = jnp.linalg.cholesky(gram_mean)
    coefficients = chol_solve(factor, moment_mean.T)
    regression = coefficients[:, 0]
    multiplier = coefficients[:, 1]
    coef_rows = coefficients.T

    def adjoint_step(block_index, running):
        value_out, state_out, flow_out, greek_acc = running
        draw_block, flow_block, taken_flag = block_inputs(block_index)
        state, path_back = jax.vjp(
            lambda spot_level, spread: path_state(draw_block, spot_level, spread),
            spot_today,
            volatility,
        )
        (basis_block, reward), feature_back = jax.vjp(
            lambda current, spot_level, spread: (
                basis_rows(current, spot_level, spread),
                payoff(current, spot_level, weights),
            ),
            state,
            spot_today,
            volatility,
        )
        fitted = lax.dot_general(
            coef_rows,
            basis_block,
            (((1,), (0,)), ((), ())),
            precision=highest,
            preferred_element_type=jnp.float32,
        )
        continuation = fitted[0]
        lam_phi = fitted[1]
        value_block = taken_flag * reward + (1.0 - taken_flag) * continuation
        rows_bar = (
            multiplier[:, None] * (flow_block - continuation)[None, :]
            + regression[:, None] * (1.0 - taken_flag - lam_phi)[None, :]
        )
        state_bar, spot_bar, spread_bar = feature_back((rows_bar, taken_flag))
        spot_path, spread_path = path_back(state_bar)
        greek_acc = greek_acc + jnp.stack([spot_bar + spot_path, spread_bar + spread_path])
        block_start = block_index * block_width
        value_out = lax.dynamic_update_slice_in_dim(value_out, value_block, block_start, 0)
        state_out = lax.dynamic_update_slice_in_dim(state_out, state_bar, block_start, 1)
        flow_out = lax.dynamic_update_slice_in_dim(flow_out, lam_phi, block_start, 0)
        return (value_out, state_out, flow_out, greek_acc)

    start_outs = (
        jnp.zeros((local_paths,), jnp.float32),
        jnp.zeros((assets, local_paths), jnp.float32),
        jnp.zeros((local_paths,), jnp.float32),
        jnp.zeros((2, assets), jnp.float32),
    )
    path_value, state_cot, flow_cot, greek_acc = lax.fori_loop(
        0, block_count, adjoint_step, start_outs
    )
    greeks = lax.psum(greek_acc, ("grp", "path")) / path_total
    return (path_value, state_cot, flow_cot, greeks)


def solution(mesh):
    in_specs = (P(None, ("grp", "path")), P(), P(), P(), P(("grp", "path")), P(("grp", "path")))
    out_specs = (P(("grp", "path")), P(None, ("grp", "path")), P(("grp", "path")), P())
    return jax.shard_map(
        per_device, mesh=mesh, in_specs=in_specs, out_specs=out_specs, check_vma=False
    )
```

profile of v0, /device:TPU:1, one launch (start us, length us, event | category | flops | bytes accessed | tf_op | source)
XLA Modules:
  0.0 799.2 jit_solution(2905008628798093460)
XLA Ops:
  7.9 80.4 %while.42 = (s32[]{:T(128)}, f32[128,128]{1,0:T(8,128)S(1)}, f32[2,128]{1,0:T(2,128)S(1)}, f32[32]{0:T(128)}, f32[32,16384]{1,0:T(8,128)}, /*index=5*/f32[32]{0:...) while((s32[]{:T(128)}, f32[128,128]{1,0:T(8,128)S(1)}, ...), condition=%wide.region_1.2_spmd.clone, body=%wide.region_0.1_spmd.clone.sunk | while | flops 204870208 | bytes 3562582 | solution.py:83
  91.7 111.2 %psum.22 = f32[2,128]{1,0:T(2,128)S(1)} all-reduce(f32[2,128]{1,0:T(2,128)S(1)} %get-tuple-element.642), channel_id=1, replica_groups=mesh['grp'=8,'path'=64] {'grp','path'}, use_global_device_ids=true, to_apply=%region_5.6 | all-reduce | flops 256 | bytes 2048 | tf_op jit(solution)/shard_map/psum | solution.py:84
  202.9 340.4 %all-reduce.5.cloned.1.call-done = f32[128,128]{0,1:T(8,128)} async-done(((f32[128,128]{0,1:T(8,128)}), f32[128,128]{0,1:T(8,128)}) %all-reduce.5.cloned.1.call-update) | async-done | bytes 65552 | tf_op jit(solution)/shard_map/psum | solution.py:84
  545.1 11.7 %cholesky.15 = f32[128,128]{1,0:T(8,128)S(1)} custom-call(f32[128,128]{1,0:T(8,128)S(1)} %fusion.19), custom_call_target="Cholesky" | custom-call | tf_op jit(solution)/shard_map/jit(cholesky)/cholesky | solution.py:87
  558.1 9.8 %custom-call.8 = f32[1,128,128]{1,2,0:T(8,128)S(1)} custom-call(f32[1,128,128]{2,1,0:T(8,128)S(1)} %fusion.14), custom_call_target="InvertDiagBlocksLowerTriangular" | custom-call | tf_op jit(solution)/shard_map/triangular_solve | solution.py:37
  568.7 121.5 %while.43 = (s32[]{:T(128)}, f32[16384]{0:T(1024)S(1)}, f32[32,16384]{1,0:T(8,128)S(1)}, f32[16384]{0:T(1024)S(1)}, f32[2,32]{1,0:T(2,128)S(1)}, /*index=5*/s32[...) while((s32[]{:T(128)}, f32[16384]{0:T(1024)S(1)}, ...), condition=%wide.region_15.16_spmd.clone, body=%wide.region_7.15_spmd.clone.sunk | while | flops 5333607 | bytes 5730625 | solution.py:139
  571.3 2.0 multiply_reduce_fusion.8
  578.9 2.0 multiply_reduce_fusion.8
  582.4 1.3 fusion.49
  586.5 2.0 multiply_reduce_fusion.8
  594.1 2.0 multiply_reduce_fusion.8
  601.7 2.0 multiply_reduce_fusion.8
  609.3 2.0 multiply_reduce_fusion.8
  616.9 2.0 multiply_reduce_fusion.8
  624.5 2.0 multiply_reduce_fusion.8
  632.1 2.0 multiply_reduce_fusion.8
  639.7 2.0 multiply_reduce_fusion.8
  647.3 2.0 multiply_reduce_fusion.8
  654.9 2.0 multiply_reduce_fusion.8
  662.5 2.0 multiply_reduce_fusion.8
  670.1 2.0 multiply_reduce_fusion.8
  677.7 2.0 multiply_reduce_fusion.8
  685.2 2.0 multiply_reduce_fusion.8
  690.3 101.5 %psum.23 = f32[2,32]{1,0:T(2,128)S(1)} all-reduce(f32[2,32]{1,0:T(2,128)S(1)} %get-tuple-element.646), channel_id=1, replica_groups=mesh['grp'=8,'path'=64] {'grp','path'}, use_global_device_ids=true, to_apply=%region_16.17 | all-reduce | flops 64 | bytes 512 | tf_op jit(solution)/shard_map/psum | solution.py:142
  (560 shorter events, 161.5 us)
Async XLA Ops:
  7.2 536.1 %all-reduce.5.cloned.1.call-start = ((), (), s32[]{:S(2)}) async-start(), calls=%async_computation | async-start | bytes 131072 | tf_op jit(solution)/shard_map/psum | solution.py:84
  7.9 81.2 %copy-start.1 = (f32[32]{0:T(128)S(1)}, f32[32]{0:T(128)}, u32[]{:S(2)}) copy-start(f32[32]{0:T(128)} %param.13) | copy-start | bytes 388
  88.3 480.4 %copy-start.2 = (f32[32]{0:T(128)S(1)}, f32[32]{0:T(128)}, u32[]{:S(2)}) copy-start(f32[32]{0:T(128)} %get-tuple-element.1153) | copy-start | bytes 388
  88.3 480.4 %copy-start.5 = (f32[32]{0:T(128)S(1)}, f32[32]{0:T(128)}, u32[]{:S(2)}) copy-start(f32[32]{0:T(128)} %get-tuple-element.1154) | copy-start | bytes 388
  690.2 102.1 %copy-start = (f32[32,16384]{1,0:T(8,128)}, f32[32,16384]{1,0:T(8,128)S(1)}, u32[]{:S(2)}) copy-start(f32[32,16384]{1,0:T(8,128)S(1)} %get-tuple-element.638) | copy-start | bytes 6291460
  690.3 102.1 %copy-start.3 = (f32[16384]{0:T(1024)}, f32[16384]{0:T(1024)S(1)}, u32[]{:S(2)}) copy-start(f32[16384]{0:T(1024)S(1)} %get-tuple-element.639) | copy-start | bytes 196612
  690.3 102.1 %copy-start.4 = (f32[16384]{0:T(1024)}, f32[16384]{0:T(1024)S(1)}, u32[]{:S(2)}) copy-start(f32[16384]{0:T(1024)S(1)} %get-tuple-element.637) | copy-start | bytes 196612
Sparse Core Ops, SparseCore 0:
  89.2 454.0 all-reduce.4
where the time goes:
time: 803 us; the launch traced here: 799 us
  waiting for transfers between devices  340 us (42%)
  blocking collectives  213 us (27%)
  other arithmetic  151 us (19%)
  local copies, waits for them, and re-layouts  40.1 us (5%)
  matrix products  24.6 us (3%)
  between operations  15.5 us (2%)
  loops' own time  14.4 us (2%)
    psum x1, waiting for transfers between devices, per_device(): gram_sum, moment_sum = lax.psum((gram_acc, moment_acc), ('grp', 'path'))  340 us
    psum x1, blocking collectives, per_device(): gram_sum, moment_sum = lax.psum((gram_acc, moment_acc), ('grp', 'path'))  111 us
    psum x1, blocking collectives, per_device(): greeks = lax.psum(greek_acc, ('grp', 'path')) / path_total  101 us
    mul x32, other arithmetic, basis_rows(): squares = (scaled * scaled - 1.0) * inv_root_two  33.1 us
    reduce_sum x16, other arithmetic, payoff(): jnp.sum(weights[:, None] * state, axis=0) / jnp.sum(weights * spot_today)  31.9 us
    concatenate x32, local copies, waits for them, and re-layouts, basis_rows(): jnp.concatenate([leading, scaled, squares, neighbour, bounded], axis=0)  21.9 us
    reduce_sum x16, other arithmetic, path_state(): volatility[:, None] * (root_time * normals)  21.4 us
  transfers between devices with their start and end apart: 1, of which 1 were waited for; matrix products, arithmetic and copies ran while one was open for 0% of the time, Pallas kernels for 0%

commit v1 on v0

v1 whole, which is shorter than its diff:
```python
import functools
import math

import jax
import jax.numpy as jnp
from jax import lax
from jax.experimental import pallas as pl
from jax.experimental.pallas import tpu as pltpu
from jax.sharding import PartitionSpec as P

MESH = pl.DeviceIdType.MESH
F32, BF16 = jnp.float32, jnp.bfloat16
expiry_time = 0.5
root_time = math.sqrt(0.5)
inv_root_two = 1.0 / math.sqrt(2.0)
root_two = math.sqrt(2.0)
notional = 20.0
soft_width = 0.02
LAST = (((1,), (1,)), ((), ()))
A = 32
N = 4 * A
GSLOTS = 9
SLOTS = 30


def column(row, size):
    eye = lax.broadcasted_iota(jnp.int32, (size, size), 0) == lax.broadcasted_iota(
        jnp.int32, (size, size), 1
    )
    return jnp.sum(jnp.where(eye, jnp.broadcast_to(row, (size, size)), 0.0), axis=1, keepdims=True)


def split(x):
    hi = x.astype(BF16)
    return hi, (x - hi.astype(F32)).astype(BF16)


def solve(g, b):
    lane = lax.broadcasted_iota(jnp.int32, (8, N), 1)
    rows = [g[8 * i : 8 * i + 8, :] for i in range(N // 8)] + [b]
    for k in range(0, N, 4):
        tile = rows[k // 8]
        pivot = []
        for q in range(4):
            r = k % 8 + q
            pivot.append(jnp.broadcast_to(tile[r : r + 1, :], (8, N)))

        def at(i, j):
            return jnp.broadcast_to(pivot[i][:, k + j : k + j + 1], (8, N))

        a, h, c = at(0, 0), at(0, 1), at(1, 1)
        b00, b01, b10, b11 = at(0, 2), at(0, 3), at(1, 2), at(1, 3)
        d00, d01, d11 = at(2, 2), at(2, 3), at(3, 3)
        inv = 1.0 / (a * c - h * h)
        i00, i01, i11 = c * inv, -(h * inv), a * inv
        e00, e01 = i00 * b00 + i01 * b10, i00 * b01 + i01 * b11
        e10, e11 = i01 * b00 + i11 * b10, i01 * b01 + i11 * b11
        s00 = d00 - (b00 * e00 + b10 * e10)
        s01 = d01 - (b00 * e01 + b10 * e11)
        s11 = d11 - (b01 * e01 + b11 * e11)
        inv = 1.0 / (s00 * s11 - s01 * s01)
        w00, w01, w11 = s11 * inv, -(s01 * inv), s00 * inv
        r0, r1, r2, r3 = (pivot[q] - (lane == k + q).astype(F32) for q in range(4))
        t2 = r2 - (e00 * r0 + e10 * r1)
        t3 = r3 - (e01 * r0 + e11 * r1)
        low0 = w00 * t2 + w01 * t3
        low1 = w01 * t2 + w11 * t3
        up0 = (i00 * r0 + i01 * r1) - (e00 * low0 + e01 * low1)
        up1 = (i01 * r0 + i11 * r1) - (e10 * low0 + e11 * low1)
        first = k // 8 if k % 8 == 0 else k // 8 + 1
        for i in range(first, N // 8 + 1):
            x = rows[i]
            c0, c1, c2, c3 = (jnp.broadcast_to(x[:, k + q : k + q + 1], (8, N)) for q in range(4))
            rows[i] = x - ((c0 * up0 + c1 * up1) + (c2 * low0 + c3 * low1))
    return rows[N // 8]


def first_kernel(
    dims, total_paths, width,
    z_hbm, spot_ref, vol_ref, wei_ref, cf_ref, ex_ref,
    s_out, t_out, rew_out, bar_out, coef_out, greek_out,
    z_ref, s_ref, t_ref, f_ref, tar_ref, q_ref,
    acc, acct, accm, accmt, accd, accv,
    pay, recv, zrecv, total,
    in_sem, out_sem, rs_send, rs_recv, z_send, z_recv, ag_send, ag_recv,
):
    local = z_ref.shape[1]
    chunks = local // width
    comm = dims is not None
    if comm:
        nx, ncore, ny, nz = dims
        plane = nx * ncore * ny
        grp, path = lax.axis_index("grp"), lax.axis_index("path")
        my_z, my_y = path // ny, path % ny
        my_x, my_core = grp // ncore, grp % ncore
        me = (my_core * ny + my_y) * nx + my_x

        def place(slot, z):
            x, y, core = slot % nx, (slot // nx) % ny, slot // (nx * ny)
            return (x * ncore + core, z * ny + y)

        barrier = pltpu.get_barrier_semaphore()

        def greet_z(d, carry):
            peer = place(me, (my_z + d) % nz)
            pl.semaphore_signal(barrier, inc=1, device_id=peer, device_id_type=MESH)
            return carry

        def greet_plane(d, carry):
            peer = place((me + d) % plane, my_z)
            pl.semaphore_signal(barrier, inc=1, device_id=peer, device_id_type=MESH)
            return carry

        lax.fori_loop(1, nz, greet_z, 0)
        lax.fori_loop(1, plane, greet_plane, 0)

    def in_copy(c):
        at = pl.ds(pl.multiple_of(c * width, width), width)
        return pltpu.make_async_copy(z_hbm.at[:, at], z_ref.at[:, at], in_sem.at[c])

    def out_copies(c):
        at = pl.ds(pl.multiple_of(c * width, width), width)
        return (
            pltpu.make_async_copy(s_ref.at[:, at], s_out.at[:, at], out_sem.at[0, c]),
            pltpu.make_async_copy(t_ref.at[:, at], t_out.at[:, at], out_sem.at[1, c]),
        )

    for c in range(chunks):
        in_copy(c).start()

    vol = column(vol_ref[...], A)
    spot = column(spot_ref[...], A)
    weight = column(wei_ref[...], A)
    spread = vol * root_time
    half = 0.5 * expiry_time * (vol * vol)
    inv_spread = 1.0 / spread
    inv_vol = 1.0 / vol
    whole = jnp.sum(weight * spot, axis=0, keepdims=True)
    share = weight * spot / whole
    row = lax.broadcasted_iota(jnp.int32, (A, width), 0)
    trow = lax.broadcasted_iota(jnp.int32, (16, width), 0)

    acc[...] = jnp.zeros_like(acc)
    acct[...] = jnp.zeros_like(acct)

    def gram_step(c, carry):
        at = pl.ds(pl.multiple_of(c * width, width), width)
        in_copy(c).wait()
        e = jnp.exp(spread * z_ref[:, at] - half)
        s = (e - 1.0) * inv_spread
        t = jnp.where(row == A - 1, 1.0, jnp.tanh(s))
        s_ref[:, at] = s
        t_ref[:, at] = t
        blocks = (s, (s * s - 1.0) * inv_root_two, s * pltpu.roll(s, A - 1, 0), t)
        for i, x in enumerate(blocks):
            hi, lo = split(x)
            f_ref[i * A : (i + 1) * A, at] = hi
            f_ref[N + i * A : N + (i + 1) * A, at] = lo
        f = f_ref[:, at]
        acc[...] += lax.dot_general(f, f, LAST, preferred_element_type=F32)
        cf = jnp.broadcast_to(cf_ref[:, at], (16, width))
        free = 1.0 - jnp.broadcast_to(ex_ref[:, at], (16, width)).astype(F32)
        c0 = cf.astype(BF16).astype(F32)
        c1 = (cf - c0).astype(BF16).astype(F32)
        c2 = cf - c0 - c1
        targets = jnp.where(
            trow == 0, c0, jnp.where(trow == 1, c1, jnp.where(trow == 2, c2, jnp.where(trow == 3, free, 0.0)))
        ).astype(BF16)
        tar_ref[:, at] = targets
        acct[...] += lax.dot_general(targets, f, LAST, preferred_element_type=F32)
        for copy in out_copies(c):
            copy.start()
        return carry

    lax.fori_loop(0, chunks, gram_step, 0)

    gram = (acc[:N, :N] + (acc[:N, N:] + acc[N:, :N])) + acc[N:, N:]
    moment = acct[:, :N] + acct[:, N:]
    lane = lax.broadcasted_iota(jnp.int32, (N // 2, N), 1)
    prow = lax.broadcasted_iota(jnp.int32, (N // 2, N), 0)
    corner = pltpu.roll(gram[N // 2 :, :], N // 2, 1)
    packed = jnp.where(lane < prow, corner, gram[: N // 2, :])
    diagonal = jnp.sum(jnp.where(lane == prow, corner, 0.0), axis=0, keepdims=True)
    for j in range(8):
        pay[j] = packed[8 * j : 8 * j + 8, :]
    r8 = lax.broadcasted_iota(jnp.int32, (8, N), 0)
    pay[8] = jnp.where(
        r8 == 0,
        moment[0:1, :] + moment[1:2, :] + moment[2:3, :],
        jnp.where(r8 == 1, moment[3:4, :], jnp.where(r8 == 2, diagonal, 0.0)),
    )

    def rs_copy(slot):
        return pltpu.make_async_remote_copy(
            src_ref=pay.at[slot], dst_ref=recv.at[me], send_sem=rs_send.at[slot], recv_sem=rs_recv.at[me],
            device_id=place(slot, my_z), device_id_type=MESH,
        )

    def rs_start(low, high):
        for slot in range(low, high):
            @pl.when(me != slot)
            def _():
                rs_copy(slot).start()

            @pl.when(me == slot)
            def _():
                recv[me] = pay[slot]

    def arrived(buffer, sem, i):
        return pltpu.make_async_remote_copy(
            src_ref=buffer.at[i], dst_ref=buffer.at[i], send_sem=rs_send.at[0], recv_sem=sem.at[i],
            device_id=place(me, my_z), device_id_type=MESH,
        )

    def z_copy(d):
        return pltpu.make_async_remote_copy(
            src_ref=zrecv.at[my_z], dst_ref=zrecv.at[my_z], send_sem=z_send.at[d], recv_sem=z_recv.at[my_z],
            device_id=place(me, (my_z + d) % nz), device_id_type=MESH,
        )

    def ag_copy(d):
        return pltpu.make_async_remote_copy(
            src_ref=total.at[me], dst_ref=total.at[me], send_sem=ag_send.at[d], recv_sem=ag_recv.at[me],
            device_id=place((me + d) % plane, my_z), device_id_type=MESH,
        )

    def z_stage():
        def wait(d, carry):
            arrived(recv, rs_recv, (me + d) % plane).wait_recv()
            return carry

        lax.fori_loop(1, plane, wait, 0)
        parts = [recv[i] for i in range(plane)]
        while len(parts) > 1:
            parts = [parts[i] + parts[i + 1] for i in range(0, len(parts), 2)]
        zrecv[my_z] = parts[0]
        for i in range(nz // 2):
            for d in ((nz // 2,) if i == 0 else (nz // 2 - i, nz // 2 + i)):
                z_copy(d).start()

    def ag_stage():
        def wait(d, carry):
            arrived(zrecv, z_recv, (my_z + d) % nz).wait_recv()
            return carry

        lax.fori_loop(1, nz, wait, 0)
        parts = [zrecv[i] for i in range(nz)]
        while len(parts) > 1:
            parts = [parts[i] + parts[i + 1] for i in range(0, len(parts), 2)]
        total[me] = parts[0]

        def send(d, carry):
            ag_copy(d).start()
            return carry

        lax.fori_loop(1, plane, send, 0)

    def ag_wait(low, high):
        def wait(slot, carry):
            @pl.when(me != slot)
            def _():
                arrived(total, ag_recv, slot).wait_recv()

            return carry

        lax.fori_loop(low, high, wait, 0)

    owns_gram = owns_rest = None
    if comm:
        owns_gram = me < GSLOTS
        owns_rest = jnp.logical_and(me >= GSLOTS, me < SLOTS)
        pl.semaphore_wait(barrier, nz - 1 + plane - 1)
        rs_start(0, GSLOTS)

    accm[...] = jnp.zeros_like(accm)
    accmt[...] = jnp.zeros_like(accmt)
    accd[...] = jnp.zeros_like(accd)
    accv[...] = jnp.zeros_like(accv)

    def adjoint_step(c, carry):
        at = pl.ds(pl.multiple_of(c * width, width), width)
        s, t = s_ref[:, at], t_ref[:, at]
        e = 1.0 + s * spread
        drift = e * (z_ref[:, at] - spread)
        q = (drift - s) * inv_vol
        for i, x in enumerate(
            (q, q * s, q * pltpu.roll(s, A - 1, 0), q * pltpu.roll(s, 1, 0), q * (1.0 - t * t))
        ):
            hi, lo = split(x)
            q_ref[i * A : (i + 1) * A, :] = hi
            q_ref[(5 + i) * A : (6 + i) * A, :] = lo
        qs = q_ref[...]
        accm[...] += lax.dot_general(qs, f_ref[:, at], LAST, preferred_element_type=F32)
        accmt[...] += lax.dot_general(qs, tar_ref[:, at], LAST, preferred_element_type=F32)
        basket = jnp.sum(share * e, axis=0, keepdims=True)
        arg = (basket - 1.0) * (1.0 / soft_width)
        small = jnp.exp(-jnp.abs(arg))
        plus = jnp.maximum(arg, 0.0) + jnp.log1p(small)
        slope = jnp.where(arg >= 0.0, 1.0, small) / (1.0 + small)
        taken = ex_ref[:, at].astype(F32)
        bar = taken * (notional * slope)
        rew_out[:, at] = taken * (notional * soft_width * plus)
        bar_out[:, at] = bar
        dd = bar * (e - basket)
        vv = bar * drift
        for j in range(width // 128):
            accd[...] += dd[:, j * 128 : (j + 1) * 128]
            accv[...] += vv[:, j * 128 : (j + 1) * 128]
        return carry

    cut = chunks
    lax.fori_loop(0, cut, adjoint_step, 0)

    rest = (accm[: 5 * A, :N] + (accm[: 5 * A, N:] + accm[5 * A :, :N])) + accm[5 * A :, N:]
    for j in range(20):
        pay[GSLOTS + j] = rest[8 * j : 8 * j + 8, :]
    lane8 = lax.broadcasted_iota(jnp.int32, (8, N), 1)
    cols = []
    dsum = jnp.sum(accd[...], axis=1, keepdims=True)
    vsum = jnp.sum(accv[...], axis=1, keepdims=True)
    mt = accmt[: 5 * A, :] + accmt[5 * A :, :]
    mcf = mt[:, 0:1] + mt[:, 1:2] + mt[:, 2:3]
    mfree = mt[:, 3:4]
    for x, count in ((dsum, 4), (vsum, 4), (mcf, 20), (mfree, 20)):
        cols += [x[8 * i : 8 * i + 8, :] for i in range(count)]
    extra = jnp.zeros((8, N), F32)
    for i, x in enumerate(cols):
        extra = jnp.where(lane8 == i, x, extra)
    pay[SLOTS - 1] = extra

    if comm:
        @pl.when(owns_gram)
        def _():
            z_stage()

        rs_start(GSLOTS, SLOTS)

        @pl.when(owns_rest)
        def _():
            z_stage()

        @pl.when(owns_gram)
        def _():
            ag_stage()

        ag_wait(0, GSLOTS)

        @pl.when(owns_rest)
        def _():
            ag_stage()
    else:
        total[...] = pay[...]

    per_path = 1.0 / total_paths
    packed = jnp.concatenate([total[j] for j in range(8)], axis=0)
    upper = jnp.where(lane > prow, packed, jnp.where(lane == prow, 0.5 * packed, 0.0))
    tail = total[8]
    lower = jnp.where(
        lane == prow, 0.5 * jnp.broadcast_to(tail[2:3, :], (N // 2, N)), jnp.where(lane < prow, packed, 0.0)
    )
    lower = pltpu.roll(jnp.where(lane < N // 2, lower, 0.0), N // 2, 1)
    folded = jnp.concatenate([upper, lower], axis=0) * per_path
    gram = folded + folded.T
    sol = solve(gram, jnp.where(r8 < 2, tail, 0.0) * per_path)
    reg, mult = sol[0:1, :], sol[1:2, :]
    big = lax.broadcasted_iota(jnp.int32, (N, N), 0)
    coef = jnp.where(big == 0, reg, jnp.where(big == 1, mult, 0.0)).T
    coef_out[...] = coef

    if comm:
        ag_wait(GSLOTS, SLOTS)
    extra = total[SLOTS - 1]
    vega = [jnp.zeros((8, 1), F32) for _ in range(4)]
    for kind in range(5):
        at = A * (kind if kind < 3 else kind - 1)
        cr, cm = coef[at : at + A, 0:1], coef[at : at + A, 1:2]
        if kind == 3:
            cr = jnp.concatenate([cr[A - 1 :], cr[: A - 1]], axis=0)
            cm = jnp.concatenate([cm[A - 1 :], cm[: A - 1]], axis=0)
        if kind == 1:
            cr, cm = cr * root_two, cm * root_two
        for i in range(4):
            j = 4 * kind + i
            block = total[GSLOTS + j]
            mr = extra[:, 8 + j : 9 + j] - jnp.sum(block * reg, axis=1, keepdims=True)
            mm = extra[:, 28 + j : 29 + j] - jnp.sum(block * mult, axis=1, keepdims=True)
            lo = 8 * i
            vega[i] = vega[i] + cm[lo : lo + 8] * mr + cr[lo : lo + 8] * mm
    delta = weight / whole * jnp.concatenate([extra[:, i : i + 1] for i in range(4)], axis=0)
    vrew = (root_time * share) * jnp.concatenate([extra[:, 4 + i : 5 + i] for i in range(4)], axis=0)
    vega = jnp.concatenate(vega, axis=0) + vrew
    glane = lax.broadcasted_iota(jnp.int32, (A, N), 1)
    both = jnp.where(glane == 0, delta, jnp.where(glane == 1, vega, 0.0)) * per_path
    both = jnp.concatenate([both, jnp.zeros((N - A, N), F32)], axis=0).T
    greek_out[...] = both[0:8, :]

    def finish(c, carry):
        for copy in out_copies(c):
            copy.wait()
        return carry

    lax.fori_loop(0, chunks, finish, 0)
    if comm:
        def sent_slot(slot, carry):
            @pl.when(me != slot)
            def _():
                rs_copy(slot).wait_send()

            return carry

        lax.fori_loop(0, SLOTS, sent_slot, 0)

        @pl.when(me < SLOTS)
        def _():
            def sent_z(d, carry):
                z_copy(d).wait_send()
                return carry

            lax.fori_loop(1, nz, sent_z, 0)

            def sent_ag(d, carry):
                ag_copy(d).wait_send()
                return carry

            lax.fori_loop(1, plane, sent_ag, 0)


def second_kernel(
    s_ref, t_ref, cf_ref, ex_ref, rew_ref, bar_ref, coef_ref, greek_ref, spot_ref, vol_ref, wei_ref,
    value_out, cot_out, flow_out, greeks,
):
    vol = column(vol_ref[...], A)
    spot = column(spot_ref[...], A)
    weight = column(wei_ref[...], A)
    scale = 1.0 / (spot * (vol * root_time))
    share = weight / jnp.sum(weight * spot, axis=0, keepdims=True)
    s, t = s_ref[...], t_ref[...]
    up, down = pltpu.roll(s, A - 1, 0), pltpu.roll(s, 1, 0)
    flat = 1.0 - t * t
    fits, bars = [], []
    for i in range(2):
        c1, c2, c3, c4 = (coef_ref[A * b : A * (b + 1), i : i + 1] for b in range(4))
        c2 = c2 * inv_root_two
        c3d = jnp.concatenate([c3[A - 1 :], c3[: A - 1]], axis=0)
        square = c2 * s
        lead = c1 + square + c3 * up
        fits.append(
            jnp.sum(s * lead + c4 * t, axis=0, keepdims=True) - jnp.sum(c2, axis=0, keepdims=True)
        )
        bars.append(lead + square + c3d * down + c4 * flat)
    taken = ex_ref[...].astype(F32)
    free = 1.0 - taken
    cont, lam = fits
    value_out[...] = rew_ref[...] + free * cont
    flow_out[...] = lam
    cot_out[...] = scale * ((cf_ref[...] - cont) * bars[1] + (free - lam) * bars[0]) + share * bar_ref[...]
    greeks[...] = greek_ref[0:2, 0:A]


def per_device(dims, total_paths, normals, spot, vol, weights, cash_flows, exercise, width=2048, width2=2048):
    local = normals.shape[1]
    chunks = local // width
    spot, vol, weights = (x.reshape(1, A) for x in (spot, vol, weights))
    cash_flows, exercise = cash_flows.reshape(1, local), exercise.reshape(1, local)
    vmem = pl.BlockSpec(memory_space=pltpu.VMEM)
    hbm = pl.BlockSpec(memory_space=pl.ANY)
    comm = dims is not None
    nz, plane = (dims[3], dims[0] * dims[1] * dims[2]) if comm else (2, 2)
    dma = pltpu.SemaphoreType.DMA
    s, t, rew, bar, coef, greek = pl.pallas_call(
        functools.partial(first_kernel, dims, total_paths, width),
        out_shape=(
            jax.ShapeDtypeStruct((A, local), F32), jax.ShapeDtypeStruct((A, local), F32),
            jax.ShapeDtypeStruct((1, local), F32), jax.ShapeDtypeStruct((1, local), F32),
            jax.ShapeDtypeStruct((N, N), F32), jax.ShapeDtypeStruct((8, N), F32),
        ),
        in_specs=[hbm] + [vmem] * 5,
        out_specs=(hbm, hbm, vmem, vmem, vmem, vmem),
        scratch_shapes=[
            pltpu.VMEM((A, local), F32), pltpu.VMEM((A, local), F32), pltpu.VMEM((A, local), F32),
            pltpu.VMEM((2 * N, local), BF16), pltpu.VMEM((16, local), BF16), pltpu.VMEM((10 * A, width), BF16),
            pltpu.VMEM((2 * N, 2 * N), F32), pltpu.VMEM((16, 2 * N), F32),
            pltpu.VMEM((10 * A, 2 * N), F32), pltpu.VMEM((10 * A, 16), F32),
            pltpu.VMEM((A, 128), F32), pltpu.VMEM((A, 128), F32),
            pltpu.VMEM((SLOTS, 8, N), F32), pltpu.VMEM((plane, 8, N), F32),
            pltpu.VMEM((nz, 8, N), F32), pltpu.VMEM((SLOTS, 8, N), F32),
            dma((chunks,)), dma((2, chunks)), dma((SLOTS,)), dma((plane,)),
            dma((nz,)), dma((nz,)), dma((plane,)), dma((SLOTS,)),
        ],
        compiler_params=pltpu.CompilerParams(
            has_side_effects=True, vmem_limit_bytes=48 * 2**20, **({"collective_id": 0} if comm else {})
        ),
        name="normal_equations",
    )(normals, spot, vol, weights, cash_flows, exercise)
    wide = pl.BlockSpec((A, width2), lambda i: (0, i))
    flat = pl.BlockSpec((1, width2), lambda i: (0, i))

    def fixed(*shape):
        return pl.BlockSpec(shape, lambda i: (0, 0))

    value, cot, flow, greeks = pl.pallas_call(
        second_kernel,
        grid=(local // width2,),
        out_shape=(
            jax.ShapeDtypeStruct((1, local), F32), jax.ShapeDtypeStruct((A, local), F32),
            jax.ShapeDtypeStruct((1, local), F32), jax.ShapeDtypeStruct((2, A), F32),
        ),
        in_specs=[wide, wide, flat, flat, flat, flat, fixed(N, N), fixed(8, N)] + [fixed(1, A)] * 3,
        out_specs=(flat, wide, flat, fixed(2, A)),
        compiler_params=pltpu.CompilerParams(vmem_limit_bytes=32 * 2**20),
        name="path_outputs",
    )(s, t, cash_flows, exercise, rew, bar, coef, greek, spot, vol, weights)
    return value.reshape(local), cot, flow.reshape(local), greeks


def solution(mesh):
    shape = dict(mesh.shape)
    ncore, ny = 2, 4
    dims = (shape["grp"] // ncore, ncore, ny, shape["path"] // ny)
    count = shape["grp"] * shape["path"]

    def body(normals, *rest):
        return per_device(dims, normals.shape[1] * count, normals, *rest)

    split_paths = ("grp", "path")
    in_specs = (P(None, split_paths), P(), P(), P(), P(split_paths), P(split_paths))
    out_specs = (P(split_paths), P(None, split_paths), P(split_paths), P())
    return jax.shard_map(body, mesh=mesh, in_specs=in_specs, out_specs=out_specs, check_vma=False)
```

time: 803 us -> 62.4 us (0.08)
  waiting for transfers between devices: 340 us -> 0 us
  blocking collectives: 213 us -> 0 us
  other arithmetic: 151 us -> 0 us
  Pallas kernels: 0 us -> 57.8 us
  local copies, waits for them, and re-layouts: 40.1 us -> 3.64 us
  matrix products: 24.6 us -> 0 us
  between operations: 15.5 us -> 0.65 us
  loops' own time: 14.4 us -> 0 us
    psum x1 -> x0, waiting for transfers between devices: 340 us -> none  [per_device(): gram_sum, moment_sum = lax.psum((gram_acc, moment_acc), ('grp', 'path'))]
    psum x2 -> x0, blocking collectives: 213 us -> none  [the longest x1 111 us: per_device(): gram_sum, moment_sum = lax.psum((gram_acc, moment_acc), ('grp', 'path'))]
    pallas_call x0 -> x2, Pallas kernels: none -> 57.8 us  [the longest x1 51.7 us: per_device(): pl.pallas_call(functools.partial(first_kernel, dims, total_paths, width),...]
    reduce_sum x32 -> x0, other arithmetic: 53.3 us -> none  [the longest x16 31.9 us: payoff(): jnp.sum(weights[:, None] * state, axis=0) / jnp.sum(weights * spot_today)]
    mul x145 -> x0, other arithmetic: 46.8 us -> none  [the longest x32 33.1 us: basis_rows(): squares = (scaled * scaled - 1.0) * inv_root_two]
    dot_general x48 -> x0, matrix products: 24.1 us -> none  [the longest x16 10.8 us: gram_step(): lax.dot_general(basis_block, basis_block, contract_last, precision=highes...]
    another operation x5 -> x0, other arithmetic: 22.9 us -> none  [the longest x3 12.4 us: per_device(): factor = jnp.linalg.cholesky(gram_mean)]
    concatenate x32 -> x0, local copies, waits for them, and re-layouts: 21.9 us -> none  [basis_rows(): jnp.concatenate([leading, scaled, squares, neighbour, bounded], axis=0)]
  transfers between devices with their start and end apart: 1 -> 0, of which waited for: 1 -> 0; matrix products, arithmetic and copies ran while one was open for 0% -> 0% of each run, Pallas kernels for 0% -> 0%
where the time goes in v1:
time: 62.4 us; the launch traced here: 62.1 us
  Pallas kernels  57.8 us (93%)
  local copies, waits for them, and re-layouts  3.64 us (6%)
  between operations  0.65 us (1%)
    pallas_call x1, Pallas kernels, per_device(): pl.pallas_call(functools.partial(first_kernel, dims, total_paths, width),...  51.7 us
    pallas_call x1, Pallas kernels, per_device(): pl.pallas_call(second_kernel, grid=(local // width2,), out_shape=(jax.Sha...  6.14 us
    unnamed x10, local copies, waits for them, and re-layouts  3.64 us

profile of v1, /device:TPU:1, one launch (start us, length us, event | category | flops | bytes accessed | tf_op | source)
XLA Modules:
  0.0 62.1 jit_solution(3697629404364010920)
XLA Ops:
  0.6 0.0 copy-start
  0.6 0.8 %copy-done = f32[16384]{0:T(1024)S(1)} copy-done((f32[16384]{0:T(1024)S(1)}, f32[16384]{0:T(1024)}, u32[]{:S(2)}) %copy-start) | copy-done | bytes 65560
  1.5 0.0 copy-start.1
  1.5 0.8 %copy-done.1 = s32[16384]{0:T(1024)S(1)} copy-done((s32[16384]{0:T(1024)S(1)}, s32[16384]{0:T(1024)}, u32[]{:S(2)}) %copy-start.1) | copy-done | bytes 65560
  2.3 0.0 copy-start.2
  2.3 0.7 %copy-done.2 = f32[32]{0:T(128)S(1)} copy-done((f32[32]{0:T(128)S(1)}, f32[32]{0:T(128)}, u32[]{:S(2)}) %copy-start.2) | copy-done | bytes 152
  3.0 0.0 copy-start.3
  3.0 0.7 %copy-done.3 = f32[32]{0:T(128)S(1)} copy-done((f32[32]{0:T(128)S(1)}, f32[32]{0:T(128)}, u32[]{:S(2)}) %copy-start.3) | copy-done | bytes 152
  3.6 0.0 copy-start.4
  3.6 0.7 %copy-done.4 = f32[32]{0:T(128)S(1)} copy-done((f32[32]{0:T(128)S(1)}, f32[32]{0:T(128)}, u32[]{:S(2)}) %copy-start.4) | copy-done | bytes 152
  4.3 51.7 %normal_equations.1 = (f32[32,16384]{1,0:T(8,128)S(1)}, f32[32,16384]{1,0:T(8,128)S(1)}, f32[1,16384]{1,0:T(1,128)S(1)}, f32[1,16384]{1,0:T(1,128)S(1)}, f32[128,128]{1,0:T(8,128)S(1)}, /*index=5*/f32[8,128]{1,0:T(8,128)S(1)}) custom-call(f32[32,16384]{1,0:T(8,128)} %z_hbm.1, f32[1,32]{1,0:T(1,128)S(1)} %bitcast.11, f32[1,32]{1,0:T(1,128)S(1)} %bitcast.13, ...), custom_call_target="tpu_custom_call" | custom-call | tf_op jit(solution)/shard_map/normal_equations/pallas_call | solution.py:470
  56.0 6.1 %path_outputs.1 = (f32[1,16384]{1,0:T(1,128)}, f32[32,16384]{1,0:T(8,128)}, f32[1,16384]{1,0:T(1,128)}, f32[2,32]{1,0:T(2,128)}) custom-call(f32[32,16384]{1,0:T(8,128)S(1)} %get-tuple-element.14.s_ref, f32[32,16384]{1,0:T(8,128)S(1)} %get-tuple-element.15.t_ref, f32[1,16384]{1,0:T(1,128)S(1)} %bitcast.8, s32[1,16384]{1,0:T(1,128)S(1)} %bitcast.10, ...), custom_call_target="tpu_custom_call" | custom-call | tf_op jit(solution)/shard_map/path_outputs/pallas_call | solution.py:501
Async XLA Ops:
  0.6 0.8 %copy-start = (f32[16384]{0:T(1024)S(1)}, f32[16384]{0:T(1024)}, u32[]{:S(2)}) copy-start(f32[16384]{0:T(1024)} %param.10) | copy-start | bytes 196612
  1.5 0.8 %copy-start.1 = (s32[16384]{0:T(1024)S(1)}, s32[16384]{0:T(1024)}, u32[]{:S(2)}) copy-start(s32[16384]{0:T(1024)} %param.11) | copy-start | bytes 196612
  2.3 0.7 %copy-start.2 = (f32[32]{0:T(128)S(1)}, f32[32]{0:T(128)}, u32[]{:S(2)}) copy-start(f32[32]{0:T(128)} %param.7) | copy-start | bytes 388
  3.0 0.7 %copy-start.3 = (f32[32]{0:T(128)S(1)}, f32[32]{0:T(128)}, u32[]{:S(2)}) copy-start(f32[32]{0:T(128)} %param.8) | copy-start | bytes 388
  3.6 0.7 %copy-start.4 = (f32[32]{0:T(128)S(1)}, f32[32]{0:T(128)}, u32[]{:S(2)}) copy-start(f32[32]{0:T(128)} %param.9) | copy-start | bytes 388

commit v2 on v1

--- a/solution.py
+++ b/solution.py
@@ -20,6 +20,7 @@
 A = 32
 N = 4 * A
 GSLOTS = 9
+SUB, SUB2 = 256, 256
 SLOTS = 30
 
 
@@ -77,12 +78,12 @@
 
 def first_kernel(
     dims, total_paths, width,
-    z_hbm, spot_ref, vol_ref, wei_ref, cf_ref, ex_ref,
-    s_out, t_out, rew_out, bar_out, coef_out, greek_out,
-    z_ref, s_ref, t_ref, f_ref, tar_ref, q_ref,
-    acc, acct, accm, accmt, accd, accv,
+    z_hbm, spot_hbm, vol_hbm, wei_hbm, cf_hbm, ex_hbm,
+    s_ref, t_ref, cf_ref, free_ref, rew_out, bar_out, coef_out, greek_out,
+    z_ref, spot_ref, vol_ref, wei_ref, ex_ref, fe_ref, fo_ref, tar_ref, q_ref, const,
+    acc, acct, accm, accc, accd, accv,
     pay, recv, zrecv, total,
-    in_sem, out_sem, rs_send, rs_recv, z_send, z_recv, ag_send, ag_recv,
+    in_sem, par_sem, rs_send, rs_recv, z_send, z_recv, ag_send, ag_recv,
 ):
     local = z_ref.shape[1]
     chunks = local // width
@@ -118,64 +119,102 @@
         at = pl.ds(pl.multiple_of(c * width, width), width)
         return pltpu.make_async_copy(z_hbm.at[:, at], z_ref.at[:, at], in_sem.at[c])
 
-    def out_copies(c):
-        at = pl.ds(pl.multiple_of(c * width, width), width)
-        return (
-            pltpu.make_async_copy(s_ref.at[:, at], s_out.at[:, at], out_sem.at[0, c]),
-            pltpu.make_async_copy(t_ref.at[:, at], t_out.at[:, at], out_sem.at[1, c]),
+    small = [
+        pltpu.make_async_copy(src, dst, par_sem.at[i])
+        for i, (src, dst) in enumerate(
+            ((spot_hbm, spot_ref), (vol_hbm, vol_ref), (wei_hbm, wei_ref), (cf_hbm, cf_ref), (ex_hbm, ex_ref))
         )
-
-    for c in range(chunks):
+    ]
+    for i in (1, 0, 2):
+        small[i].start()
+    in_copy(0).start()
+    small[3].start()
+    small[4].start()
+    for c in range(1, chunks):
         in_copy(c).start()
+    for i in range(3):
+        small[i].wait()
 
     vol = column(vol_ref[...], A)
     spot = column(spot_ref[...], A)
     weight = column(wei_ref[...], A)
     spread = vol * root_time
-    half = 0.5 * expiry_time * (vol * vol)
-    inv_spread = 1.0 / spread
-    inv_vol = 1.0 / vol
     whole = jnp.sum(weight * spot, axis=0, keepdims=True)
     share = weight * spot / whole
-    row = lax.broadcasted_iota(jnp.int32, (A, width), 0)
-    trow = lax.broadcasted_iota(jnp.int32, (16, width), 0)
+    for i, x in enumerate(
+        (spread, 0.5 * expiry_time * (vol * vol), 1.0 / spread, 1.0 / vol, share)
+    ):
+        const[i] = jnp.broadcast_to(x, (A, 128))
+
+    def wide(i):
+        x = const[i]
+        return jnp.concatenate([x] * (SUB // 128), axis=1)
+
+    row = lax.broadcasted_iota(jnp.int32, (A, SUB), 0)
+    trow = lax.broadcasted_iota(jnp.int32, (16, SUB), 0)
 
     acc[...] = jnp.zeros_like(acc)
     acct[...] = jnp.zeros_like(acct)
-
-    def gram_step(c, carry):
+    small[3].wait()
+    small[4].wait()
+
+    def basis(c, f_ref, half):
+        in_copy(c).wait()
+        for b in range(width // SUB):
+            at = pl.ds(pl.multiple_of(c * width + b * SUB, SUB), SUB)
+            to = pl.ds(pl.multiple_of(half * width + b * SUB, SUB), SUB)
+            e = jnp.exp(wide(0) * z_ref[:, at] - wide(1))
+            s = (e - 1.0) * wide(2)
+            t = jnp.where(row == A - 1, 1.0, jnp.tanh(s))
+            s_ref[:, at] = s
+            t_ref[:, at] = t
+            free = 1.0 - ex_ref[:, at].astype(F32)
+            free_ref[:, at] = free
+            blocks = (s, (s * s - 1.0) * inv_root_two, s * pltpu.roll(s, A - 1, 0), t)
+            for i, x in enumerate(blocks):
+                hi, lo = split(x)
+                if i == 3:
+                    lo = (x - hi.astype(F32))
+                    lo = jnp.where(row == A - 1, jnp.broadcast_to(free, (A, SUB)), lo).astype(BF16)
+                f_ref[i * A : (i + 1) * A, to] = hi
+                f_ref[N + i * A : N + (i + 1) * A, to] = lo
+            cf = jnp.broadcast_to(cf_ref[:, at], (16, SUB))
+            c0 = cf.astype(BF16).astype(F32)
+            c1 = (cf - c0).astype(BF16).astype(F32)
+            c2 = cf - c0 - c1
+            tar_ref[:, at] = jnp.where(
+                trow == 0, c0, jnp.where(trow == 1, c1, jnp.where(trow == 2, c2, 0.0))
+            ).astype(BF16)
+
+    def gram_dot(c, f_ref, half):
+        f = f_ref[:, pl.ds(pl.multiple_of(half * width, width), width)]
+        acc[...] += lax.dot_general(f, f, LAST, preferred_element_type=F32)
         at = pl.ds(pl.multiple_of(c * width, width), width)
-        in_copy(c).wait()
-        e = jnp.exp(spread * z_ref[:, at] - half)
-        s = (e - 1.0) * inv_spread
-        t = jnp.where(row == A - 1, 1.0, jnp.tanh(s))
-        s_ref[:, at] = s
-        t_ref[:, at] = t
-        blocks = (s, (s * s - 1.0) * inv_root_two, s * pltpu.roll(s, A - 1, 0), t)
-        for i, x in enumerate(blocks):
-            hi, lo = split(x)
-            f_ref[i * A : (i + 1) * A, at] = hi
-            f_ref[N + i * A : N + (i + 1) * A, at] = lo
-        f = f_ref[:, at]
-        acc[...] += lax.dot_general(f, f, LAST, preferred_element_type=F32)
-        cf = jnp.broadcast_to(cf_ref[:, at], (16, width))
-        free = 1.0 - jnp.broadcast_to(ex_ref[:, at], (16, width)).astype(F32)
-        c0 = cf.astype(BF16).astype(F32)
-        c1 = (cf - c0).astype(BF16).astype(F32)
-        c2 = cf - c0 - c1
-        targets = jnp.where(
-            trow == 0, c0, jnp.where(trow == 1, c1, jnp.where(trow == 2, c2, jnp.where(trow == 3, free, 0.0)))
-        ).astype(BF16)
-        tar_ref[:, at] = targets
-        acct[...] += lax.dot_general(targets, f, LAST, preferred_element_type=F32)
-        for copy in out_copies(c):
-            copy.start()
+        acct[...] += lax.dot_general(tar_ref[:, at], f, LAST, preferred_element_type=F32)
+
+    pairs = chunks // 2
+    basis(0, fe_ref, 0)
+
+    def gram_step(i, carry):
+        basis(2 * i + 1, fo_ref, i)
+        gram_dot(2 * i, fe_ref, i)
+        basis(2 * i + 2, fe_ref, i + 1)
+        gram_dot(2 * i + 1, fo_ref, i)
         return carry
 
-    lax.fori_loop(0, chunks, gram_step, 0)
-
-    gram = (acc[:N, :N] + (acc[:N, N:] + acc[N:, :N])) + acc[N:, N:]
-    moment = acct[:, :N] + acct[:, N:]
+    lax.fori_loop(0, pairs - 1, gram_step, 0)
+    basis(chunks - 1, fo_ref, pairs - 1)
+    gram_dot(chunks - 2, fe_ref, pairs - 1)
+    gram_dot(chunks - 1, fo_ref, pairs - 1)
+
+    low_row = lax.broadcasted_iota(jnp.int32, (N, N), 0) < N - 1
+    low_col = lax.broadcasted_iota(jnp.int32, (N, N), 1) < N - 1
+    cross = jnp.where(low_col, acc[:N, N:], 0.0) + jnp.where(low_row, acc[N:, :N], 0.0)
+    gram = (acc[:N, :N] + cross) + jnp.where(jnp.logical_and(low_row, low_col), acc[N:, N:], 0.0)
+    lane1 = lax.broadcasted_iota(jnp.int32, (16, N), 1)
+    moment = acct[:, :N] + jnp.where(lane1 < N - 1, acct[:, N:], 0.0)
+    lane1 = lax.broadcasted_iota(jnp.int32, (1, N), 1)
+    moment_free = acc[2 * N - 1 :, :N] + jnp.where(lane1 < N - 1, acc[2 * N - 1 :, N:], 0.0)
     lane = lax.broadcasted_iota(jnp.int32, (N // 2, N), 1)
     prow = lax.broadcasted_iota(jnp.int32, (N // 2, N), 0)
     corner = pltpu.roll(gram[N // 2 :, :], N // 2, 1)
@@ -187,7 +226,7 @@
     pay[8] = jnp.where(
         r8 == 0,
         moment[0:1, :] + moment[1:2, :] + moment[2:3, :],
-        jnp.where(r8 == 1, moment[3:4, :], jnp.where(r8 == 2, diagonal, 0.0)),
+        jnp.where(r8 == 1, moment_free, jnp.where(r8 == 2, diagonal, 0.0)),
     )
 
     def rs_copy(slot):
@@ -273,54 +312,82 @@
         rs_start(0, GSLOTS)
 
     accm[...] = jnp.zeros_like(accm)
-    accmt[...] = jnp.zeros_like(accmt)
+    accc[...] = jnp.zeros_like(accc)
     accd[...] = jnp.zeros_like(accd)
     accv[...] = jnp.zeros_like(accv)
 
-    def adjoint_step(c, carry):
-        at = pl.ds(pl.multiple_of(c * width, width), width)
-        s, t = s_ref[:, at], t_ref[:, at]
-        e = 1.0 + s * spread
-        drift = e * (z_ref[:, at] - spread)
-        q = (drift - s) * inv_vol
-        for i, x in enumerate(
-            (q, q * s, q * pltpu.roll(s, A - 1, 0), q * pltpu.roll(s, 1, 0), q * (1.0 - t * t))
-        ):
-            hi, lo = split(x)
-            q_ref[i * A : (i + 1) * A, :] = hi
-            q_ref[(5 + i) * A : (6 + i) * A, :] = lo
-        qs = q_ref[...]
-        accm[...] += lax.dot_general(qs, f_ref[:, at], LAST, preferred_element_type=F32)
-        accmt[...] += lax.dot_general(qs, tar_ref[:, at], LAST, preferred_element_type=F32)
-        basket = jnp.sum(share * e, axis=0, keepdims=True)
-        arg = (basket - 1.0) * (1.0 / soft_width)
-        small = jnp.exp(-jnp.abs(arg))
-        plus = jnp.maximum(arg, 0.0) + jnp.log1p(small)
-        slope = jnp.where(arg >= 0.0, 1.0, small) / (1.0 + small)
-        taken = ex_ref[:, at].astype(F32)
-        bar = taken * (notional * slope)
-        rew_out[:, at] = taken * (notional * soft_width * plus)
-        bar_out[:, at] = bar
-        dd = bar * (e - basket)
-        vv = bar * drift
-        for j in range(width // 128):
-            accd[...] += dd[:, j * 128 : (j + 1) * 128]
-            accv[...] += vv[:, j * 128 : (j + 1) * 128]
+    def adjoint(c, slot):
+        sums = [jnp.zeros((A, SUB), F32) for _ in range(7)]
+        for b in range(width // SUB):
+            at = pl.ds(pl.multiple_of(c * width + b * SUB, SUB), SUB)
+            to = pl.ds(b * SUB, SUB)
+            s, t = s_ref[:, at], t_ref[:, at]
+            spread = wide(0)
+            e = 1.0 + s * spread
+            drift = e * (z_ref[:, at] - spread)
+            q = (drift - s) * wide(3)
+            cf = cf_ref[:, at]
+            for i, x in enumerate(
+                (q, q * s, q * pltpu.roll(s, A - 1, 0), q * pltpu.roll(s, 1, 0), q * (1.0 - t * t))
+            ):
+                hi, lo = split(x)
+                q_ref[slot, i * A : (i + 1) * A, to] = hi
+                q_ref[slot, (5 + i) * A : (6 + i) * A, to] = lo
+                sums[i] = sums[i] + x * cf
+            basket = jnp.sum(wide(4) * e, axis=0, keepdims=True)
+            arg = (basket - 1.0) * (1.0 / soft_width)
+            tiny = jnp.exp(-jnp.abs(arg))
+            plus = jnp.maximum(arg, 0.0) + jnp.log1p(tiny)
+            slope = jnp.where(arg >= 0.0, 1.0, tiny) / (1.0 + tiny)
+            taken = 1.0 - free_ref[:, at]
+            bar = taken * (notional * slope)
+            rew_out[:, at] = taken * (notional * soft_width * plus)
+            bar_out[:, at] = bar
+            sums[5] = sums[5] + bar * (e - basket)
+            sums[6] = sums[6] + bar * drift
+        for i, x in enumerate(sums):
+            folded = x[:, :128]
+            for j in range(1, SUB // 128):
+                folded = folded + x[:, j * 128 : (j + 1) * 128]
+            if i < 5:
+                accc[i * A : (i + 1) * A, :] += folded
+            else:
+                (accd, accv)[i - 5][...] += folded
+
+    def rest_dot(slot, f_ref, half):
+        f = f_ref[:, pl.ds(pl.multiple_of(half * width, width), width)]
+        accm[...] += lax.dot_general(q_ref[slot], f, LAST, preferred_element_type=F32)
+
+    def adjoint_step(i, carry):
+        adjoint(2 * i + 1, 1)
+        rest_dot(0, fe_ref, i)
+        adjoint(2 * i + 2, 0)
+        rest_dot(1, fo_ref, i)
         return carry
 
-    cut = chunks
+    adjoint(0, 0)
+    cut = pairs - 1
     lax.fori_loop(0, cut, adjoint_step, 0)
-
-    rest = (accm[: 5 * A, :N] + (accm[: 5 * A, N:] + accm[5 * A :, :N])) + accm[5 * A :, N:]
+    if comm:
+        @pl.when(owns_gram)
+        def _():
+            z_stage()
+
+    adjoint(chunks - 1, 1)
+    rest_dot(0, fe_ref, pairs - 1)
+    rest_dot(1, fo_ref, pairs - 1)
+
+    lowl = lax.broadcasted_iota(jnp.int32, (5 * A, N), 1) < N - 1
+    right = accm[: 5 * A, N:] + accm[5 * A :, N:]
+    rest = (accm[: 5 * A, :N] + accm[5 * A :, :N]) + jnp.where(lowl, right, 0.0)
+    mfree = right[:, N - 1 : N]
     for j in range(20):
         pay[GSLOTS + j] = rest[8 * j : 8 * j + 8, :]
     lane8 = lax.broadcasted_iota(jnp.int32, (8, N), 1)
     cols = []
     dsum = jnp.sum(accd[...], axis=1, keepdims=True)
     vsum = jnp.sum(accv[...], axis=1, keepdims=True)
-    mt = accmt[: 5 * A, :] + accmt[5 * A :, :]
-    mcf = mt[:, 0:1] + mt[:, 1:2] + mt[:, 2:3]
-    mfree = mt[:, 3:4]
+    mcf = jnp.sum(accc[...], axis=1, keepdims=True)
     for x, count in ((dsum, 4), (vsum, 4), (mcf, 20), (mfree, 20)):
         cols += [x[8 * i : 8 * i + 8, :] for i in range(count)]
     extra = jnp.zeros((8, N), F32)
@@ -329,10 +396,6 @@
     pay[SLOTS - 1] = extra
 
     if comm:
-        @pl.when(owns_gram)
-        def _():
-            z_stage()
-
         rs_start(GSLOTS, SLOTS)
 
         @pl.when(owns_rest)
@@ -394,12 +457,6 @@
     both = jnp.concatenate([both, jnp.zeros((N - A, N), F32)], axis=0).T
     greek_out[...] = both[0:8, :]
 
-    def finish(c, carry):
-        for copy in out_copies(c):
-            copy.wait()
-        return carry
-
-    lax.fori_loop(0, chunks, finish, 0)
     if comm:
         def sent_slot(slot, carry):
             @pl.when(me != slot)
@@ -426,90 +483,142 @@
 
 
 def second_kernel(
-    s_ref, t_ref, cf_ref, ex_ref, rew_ref, bar_ref, coef_ref, greek_ref, spot_ref, vol_ref, wei_ref,
-    value_out, cot_out, flow_out, greeks,
+    width, s_ref, t_ref, cf_ref, free_ref, rew_ref, bar_ref, coef_ref, greek_ref, spot_hbm, vol_hbm, wei_hbm,
+    value_hbm, cot_hbm, flow_hbm, greek_hbm,
+    spot_ref, vol_ref, wei_ref, const, value_ref, cot_ref, flow_ref, greeks, par_sem, out_sem,
 ):
+    local = s_ref.shape[1]
+    chunks = local // width
+    small = [
+        pltpu.make_async_copy(src, dst, par_sem.at[i])
+        for i, (src, dst) in enumerate(((spot_hbm, spot_ref), (vol_hbm, vol_ref), (wei_hbm, wei_ref)))
+    ]
+    for copy in small:
+        copy.start()
+
+    def outs(c):
+        at = pl.ds(pl.multiple_of(c * width, width), width)
+        return [
+            pltpu.make_async_copy(src.at[:, at], dst.at[:, at], out_sem.at[i, c])
+            for i, (src, dst) in enumerate(((cot_ref, cot_hbm), (value_ref, value_hbm), (flow_ref, flow_hbm)))
+        ]
+
+    offsets = []
+    for i in range(2):
+        c1, c2, c3, c4 = (coef_ref[A * b : A * (b + 1), i : i + 1] for b in range(4))
+        c2 = c2 * inv_root_two
+        c3d = jnp.concatenate([c3[A - 1 :], c3[: A - 1]], axis=0)
+        for j, x in enumerate((c1, c2, c3, c3d, c4)):
+            const[5 * i + j] = jnp.broadcast_to(x, (A, 128))
+        offsets.append(jnp.sum(c2, axis=0, keepdims=True))
+    greeks[...] = greek_ref[0:2, 0:A]
+    last = pltpu.make_async_copy(greeks, greek_hbm, par_sem.at[3])
+    last.start()
+    for copy in small:
+        copy.wait()
     vol = column(vol_ref[...], A)
     spot = column(spot_ref[...], A)
     weight = column(wei_ref[...], A)
     scale = 1.0 / (spot * (vol * root_time))
     share = weight / jnp.sum(weight * spot, axis=0, keepdims=True)
-    s, t = s_ref[...], t_ref[...]
-    up, down = pltpu.roll(s, A - 1, 0), pltpu.roll(s, 1, 0)
-    flat = 1.0 - t * t
-    fits, bars = [], []
-    for i in range(2):
-        c1, c2, c3, c4 = (coef_ref[A * b : A * (b + 1), i : i + 1] for b in range(4))
-        c2 = c2 * inv_root_two
-        c3d = jnp.concatenate([c3[A - 1 :], c3[: A - 1]], axis=0)
-        square = c2 * s
-        lead = c1 + square + c3 * up
-        fits.append(
-            jnp.sum(s * lead + c4 * t, axis=0, keepdims=True) - jnp.sum(c2, axis=0, keepdims=True)
-        )
-        bars.append(lead + square + c3d * down + c4 * flat)
-    taken = ex_ref[...].astype(F32)
-    free = 1.0 - taken
-    cont, lam = fits
-    value_out[...] = rew_ref[...] + free * cont
-    flow_out[...] = lam
-    cot_out[...] = scale * ((cf_ref[...] - cont) * bars[1] + (free - lam) * bars[0]) + share * bar_ref[...]
-    greeks[...] = greek_ref[0:2, 0:A]
+    const[10] = jnp.broadcast_to(scale, (A, 128))
+    const[11] = jnp.broadcast_to(share, (A, 128))
+
+    def wide(i):
+        x = const[i]
+        return jnp.concatenate([x] * (SUB2 // 128), axis=1)
+
+    def step(c, carry):
+        for b in range(width // SUB2):
+            at = pl.ds(pl.multiple_of(c * width + b * SUB2, SUB2), SUB2)
+            s, t = s_ref[:, at], t_ref[:, at]
+            up, down = pltpu.roll(s, A - 1, 0), pltpu.roll(s, 1, 0)
+            flat = 1.0 - t * t
+            fits, bars = [], []
+            for i in range(2):
+                square = wide(5 * i + 1) * s
+                lead = wide(5 * i) + square + wide(5 * i + 2) * up
+                c4 = wide(5 * i + 4)
+                fits.append(jnp.sum(s * lead + c4 * t, axis=0, keepdims=True) - offsets[i])
+                bars.append(lead + square + wide(5 * i + 3) * down + c4 * flat)
+            free = free_ref[:, at]
+            cont, lam = fits
+            value_ref[:, at] = rew_ref[:, at] + free * cont
+            flow_ref[:, at] = lam
+            cot_ref[:, at] = (
+                wide(10) * ((cf_ref[:, at] - cont) * bars[1] + (free - lam) * bars[0]) + wide(11) * bar_ref[:, at]
+            )
+        for copy in outs(c):
+            copy.start()
+        return carry
+
+    lax.fori_loop(0, chunks, step, 0)
+
+    def finish(c, carry):
+        for copy in outs(c):
+            copy.wait()
+        return carry
+
+    lax.fori_loop(0, chunks, finish, 0)
+    last.wait()
 
 
 def per_device(dims, total_paths, normals, spot, vol, weights, cash_flows, exercise, width=2048, width2=2048):
+    comm = dims is not None
     local = normals.shape[1]
     chunks = local // width
     spot, vol, weights = (x.reshape(1, A) for x in (spot, vol, weights))
     cash_flows, exercise = cash_flows.reshape(1, local), exercise.reshape(1, local)
+    if comm:
+        normals, spot, vol, weights, cash_flows, exercise = (
+            pltpu.with_memory_space_constraint(x, pltpu.HBM)
+            for x in (normals, spot, vol, weights, cash_flows, exercise)
+        )
     vmem = pl.BlockSpec(memory_space=pltpu.VMEM)
-    hbm = pl.BlockSpec(memory_space=pl.ANY)
-    comm = dims is not None
+    hbm = pl.BlockSpec(memory_space=pltpu.HBM)
     nz, plane = (dims[3], dims[0] * dims[1] * dims[2]) if comm else (2, 2)
     dma = pltpu.SemaphoreType.DMA
-    s, t, rew, bar, coef, greek = pl.pallas_call(
+    wide, flat = jax.ShapeDtypeStruct((A, local), F32), jax.ShapeDtypeStruct((1, local), F32)
+    half = pltpu.VMEM((2 * N, local // 2), BF16)
+    tiny = pltpu.VMEM((1, A), F32)
+    *arrays, coef, greek = pl.pallas_call(
         functools.partial(first_kernel, dims, total_paths, width),
         out_shape=(
-            jax.ShapeDtypeStruct((A, local), F32), jax.ShapeDtypeStruct((A, local), F32),
-            jax.ShapeDtypeStruct((1, local), F32), jax.ShapeDtypeStruct((1, local), F32),
+            wide, wide, flat, flat, flat, flat,
             jax.ShapeDtypeStruct((N, N), F32), jax.ShapeDtypeStruct((8, N), F32),
         ),
-        in_specs=[hbm] + [vmem] * 5,
-        out_specs=(hbm, hbm, vmem, vmem, vmem, vmem),
+        in_specs=[hbm] * 6,
+        out_specs=(vmem,) * 8,
         scratch_shapes=[
-            pltpu.VMEM((A, local), F32), pltpu.VMEM((A, local), F32), pltpu.VMEM((A, local), F32),
-            pltpu.VMEM((2 * N, local), BF16), pltpu.VMEM((16, local), BF16), pltpu.VMEM((10 * A, width), BF16),
+            pltpu.VMEM((A, local), F32), tiny, tiny, tiny, pltpu.VMEM((1, local), jnp.int32),
+            half, half, pltpu.VMEM((16, local), BF16), pltpu.VMEM((2, 10 * A, width), BF16),
+            pltpu.VMEM((5, A, 128), F32),
             pltpu.VMEM((2 * N, 2 * N), F32), pltpu.VMEM((16, 2 * N), F32),
-            pltpu.VMEM((10 * A, 2 * N), F32), pltpu.VMEM((10 * A, 16), F32),
+            pltpu.VMEM((10 * A, 2 * N), F32), pltpu.VMEM((5 * A, 128), F32),
             pltpu.VMEM((A, 128), F32), pltpu.VMEM((A, 128), F32),
             pltpu.VMEM((SLOTS, 8, N), F32), pltpu.VMEM((plane, 8, N), F32),
             pltpu.VMEM((nz, 8, N), F32), pltpu.VMEM((SLOTS, 8, N), F32),
-            dma((chunks,)), dma((2, chunks)), dma((SLOTS,)), dma((plane,)),
+            dma((chunks,)), dma((5,)), dma((SLOTS,)), dma((plane,)),
             dma((nz,)), dma((nz,)), dma((plane,)), dma((SLOTS,)),
         ],
         compiler_params=pltpu.CompilerParams(
-            has_side_effects=True, vmem_limit_bytes=48 * 2**20, **({"collective_id": 0} if comm else {})
+            has_side_effects=True, vmem_limit_bytes=40 * 2**20, **({"collective_id": 0} if comm else {})
         ),
         name="normal_equations",
     )(normals, spot, vol, weights, cash_flows, exercise)
-    wide = pl.BlockSpec((A, width2), lambda i: (0, i))
-    flat = pl.BlockSpec((1, width2), lambda i: (0, i))
-
-    def fixed(*shape):
-        return pl.BlockSpec(shape, lambda i: (0, 0))
-
     value, cot, flow, greeks = pl.pallas_call(
-        second_kernel,
-        grid=(local // width2,),
-        out_shape=(
-            jax.ShapeDtypeStruct((1, local), F32), jax.ShapeDtypeStruct((A, local), F32),
-            jax.ShapeDtypeStruct((1, local), F32), jax.ShapeDtypeStruct((2, A), F32),
-        ),
-        in_specs=[wide, wide, flat, flat, flat, flat, fixed(N, N), fixed(8, N)] + [fixed(1, A)] * 3,
-        out_specs=(flat, wide, flat, fixed(2, A)),
+        functools.partial(second_kernel, width2),
+        out_shape=(flat, wide, flat, jax.ShapeDtypeStruct((2, A), F32)),
+        in_specs=[vmem] * 8 + [hbm] * 3,
+        out_specs=(hbm,) * 4,
+        scratch_shapes=[
+            tiny, tiny, tiny, pltpu.VMEM((12, A, 128), F32),
+            pltpu.VMEM((1, local), F32), pltpu.VMEM((A, local), F32), pltpu.VMEM((1, local), F32),
+            pltpu.VMEM((2, A), F32), dma((4,)), dma((3, local // width2)),
+        ],
         compiler_params=pltpu.CompilerParams(vmem_limit_bytes=32 * 2**20),
         name="path_outputs",
-    )(s, t, cash_flows, exercise, rew, bar, coef, greek, spot, vol, weights)
+    )(*arrays, coef, greek, spot, vol, weights)
     return value.reshape(local), cot, flow.reshape(local), greeks
 
 

time: 62.4 us -> 57.3 us (0.918)
  local copies, waits for them, and re-layouts: 3.64 us -> 0 us
  Pallas kernels: 57.8 us -> 56.5 us
    unnamed x10 -> x0, local copies, waits for them, and re-layouts: 3.64 us -> none
    pallas_call x1, Pallas kernels: 6.14 us -> 5.18 us  [per_device(): pl.pallas_call(functools.partial(second_kernel, width2), out_shape=(flat,...]
where the time goes in v2:
time: 57.3 us; the launch traced here: 57.1 us
  Pallas kernels  56.5 us (99%)
  between operations  0.64 us (1%)
    pallas_call x1, Pallas kernels, per_device(): pl.pallas_call(functools.partial(first_kernel, dims, total_paths, width),...  51.3 us
    pallas_call x1, Pallas kernels, per_device(): pl.pallas_call(functools.partial(second_kernel, width2), out_shape=(flat,...  5.18 us

profile of v2, /device:TPU:1, one launch (start us, length us, event | category | flops | bytes accessed | tf_op | source)
XLA Modules:
  0.0 57.1 jit_solution(6949359965286791937)
XLA Ops:
  0.6 51.3 %normal_equations.1 = (f32[32,16384]{1,0:T(8,128)S(1)}, f32[32,16384]{1,0:T(8,128)S(1)}, f32[1,16384]{1,0:T(1,128)S(1)}, f32[1,16384]{1,0:T(1,128)S(1)}, f32[1,1...) custom-call(f32[32,16384]{1,0:T(8,128)} %z_hbm.1, f32[1,32]{1,0:T(1,128)} %bitcast.9, ...), custom_call_target="tpu_custom_call" | custom-call | tf_op jit(solution)/shard_map/normal_equations/pallas_call | solution.py:584
  52.0 5.2 %path_outputs.1 = (f32[1,16384]{1,0:T(1,128)}, f32[32,16384]{1,0:T(8,128)}, f32[1,16384]{1,0:T(1,128)}, f32[2,32]{1,0:T(2,128)}) custom-call(f32[32,16384]{1,0:T(8,128)S(1)} %get-tuple-element.16.s_ref, f32[32,16384]{1,0:T(8,128)S(1)} %get-tuple-element.17.t_ref, f32[1,16384]{1,0:T(1,128)S(1)} %get-tuple-element.18.cf_ref, ...), custom_call_target="tpu_custom_call" | custom-call | tf_op jit(solution)/shard_map/path_outputs/pallas_call | solution.py:609

commit v3 on v2

--- a/solution.py
+++ b/solution.py
@@ -20,7 +20,7 @@
 A = 32
 N = 4 * A
 GSLOTS = 9
-SUB, SUB2 = 256, 256
+SUB = 256
 SLOTS = 30
 
 
@@ -36,10 +36,12 @@
     return hi, (x - hi.astype(F32)).astype(BF16)
 
 
-def solve(g, b):
+def solve(g, b, between):
     lane = lax.broadcasted_iota(jnp.int32, (8, N), 1)
     rows = [g[8 * i : 8 * i + 8, :] for i in range(N // 8)] + [b]
     for k in range(0, N, 4):
+        if k == N // 2:
+            between()
         tile = rows[k // 8]
         pivot = []
         for q in range(4):
@@ -79,8 +81,8 @@
 def first_kernel(
     dims, total_paths, width,
     z_hbm, spot_hbm, vol_hbm, wei_hbm, cf_hbm, ex_hbm,
-    s_ref, t_ref, cf_ref, free_ref, rew_out, bar_out, coef_out, greek_out,
-    z_ref, spot_ref, vol_ref, wei_ref, ex_ref, fe_ref, fo_ref, tar_ref, q_ref, const,
+    value_ref, cot_ref, flow_ref, greek_out,
+    s_ref, t_ref, up_ref, down_ref, flat_ref, cf_ref, free_ref, rew_ref, bar_ref, z_ref, spot_ref, vol_ref, wei_ref, ex_ref, fe_ref, fo_ref, tar_ref, q_ref, const,
     acc, acct, accm, accc, accd, accv,
     pay, recv, zrecv, total,
     in_sem, par_sem, rs_send, rs_recv, z_send, z_recv, ag_send, ag_recv,
@@ -142,7 +144,7 @@
     whole = jnp.sum(weight * spot, axis=0, keepdims=True)
     share = weight * spot / whole
     for i, x in enumerate(
-        (spread, 0.5 * expiry_time * (vol * vol), 1.0 / spread, 1.0 / vol, share)
+        (spread, 0.5 * expiry_time * (vol * vol), 1.0 / spread, 1.0 / vol, share, 1.0 / (spot * spread), weight / whole)
     ):
         const[i] = jnp.broadcast_to(x, (A, 128))
 
@@ -322,13 +324,17 @@
             at = pl.ds(pl.multiple_of(c * width + b * SUB, SUB), SUB)
             to = pl.ds(b * SUB, SUB)
             s, t = s_ref[:, at], t_ref[:, at]
+            up, down, flat = pltpu.roll(s, A - 1, 0), pltpu.roll(s, 1, 0), 1.0 - t * t
+            up_ref[:, at] = up
+            down_ref[:, at] = down
+            flat_ref[:, at] = flat
             spread = wide(0)
             e = 1.0 + s * spread
             drift = e * (z_ref[:, at] - spread)
             q = (drift - s) * wide(3)
             cf = cf_ref[:, at]
             for i, x in enumerate(
-                (q, q * s, q * pltpu.roll(s, A - 1, 0), q * pltpu.roll(s, 1, 0), q * (1.0 - t * t))
+                (q, q * s, q * up, q * down, q * flat)
             ):
                 hi, lo = split(x)
                 q_ref[slot, i * A : (i + 1) * A, to] = hi
@@ -341,8 +347,8 @@
             slope = jnp.where(arg >= 0.0, 1.0, tiny) / (1.0 + tiny)
             taken = 1.0 - free_ref[:, at]
             bar = taken * (notional * slope)
-            rew_out[:, at] = taken * (notional * soft_width * plus)
-            bar_out[:, at] = bar
+            rew_ref[:, at] = taken * (notional * soft_width * plus)
+            bar_ref[:, at] = bar
             sums[5] = sums[5] + bar * (e - basket)
             sums[6] = sums[6] + bar * drift
         for i, x in enumerate(sums):
@@ -359,6 +365,11 @@
         accm[...] += lax.dot_general(q_ref[slot], f, LAST, preferred_element_type=F32)
 
     def adjoint_step(i, carry):
+        if comm:
+            @pl.when(jnp.logical_and(owns_gram, i == pairs // 2))
+            def _():
+                z_stage()
+
         adjoint(2 * i + 1, 1)
         rest_dot(0, fe_ref, i)
         adjoint(2 * i + 2, 0)
@@ -366,13 +377,7 @@
         return carry
 
     adjoint(0, 0)
-    cut = pairs - 1
-    lax.fori_loop(0, cut, adjoint_step, 0)
-    if comm:
-        @pl.when(owns_gram)
-        def _():
-            z_stage()
-
+    lax.fori_loop(0, pairs - 1, adjoint_step, 0)
     adjoint(chunks - 1, 1)
     rest_dot(0, fe_ref, pairs - 1)
     rest_dot(1, fo_ref, pairs - 1)
@@ -407,10 +412,6 @@
             ag_stage()
 
         ag_wait(0, GSLOTS)
-
-        @pl.when(owns_rest)
-        def _():
-            ag_stage()
     else:
         total[...] = pay[...]
 
@@ -424,11 +425,49 @@
     lower = pltpu.roll(jnp.where(lane < N // 2, lower, 0.0), N // 2, 1)
     folded = jnp.concatenate([upper, lower], axis=0) * per_path
     gram = folded + folded.T
-    sol = solve(gram, jnp.where(r8 < 2, tail, 0.0) * per_path)
+
+    def between():
+        if comm:
+            @pl.when(owns_rest)
+            def _():
+                ag_stage()
+
+    sol = solve(gram, jnp.where(r8 < 2, tail, 0.0) * per_path, between)
     reg, mult = sol[0:1, :], sol[1:2, :]
     big = lax.broadcasted_iota(jnp.int32, (N, N), 0)
     coef = jnp.where(big == 0, reg, jnp.where(big == 1, mult, 0.0)).T
-    coef_out[...] = coef
+
+    offsets = []
+    for i in range(2):
+        c1, c2, c3, c4 = (coef[A * b : A * (b + 1), i : i + 1] for b in range(4))
+        c2 = c2 * inv_root_two
+        c3d = jnp.concatenate([c3[A - 1 :], c3[: A - 1]], axis=0)
+        for j, x in enumerate((c1, c2, c3, c3d, c4)):
+            const[7 + 5 * i + j] = jnp.broadcast_to(x, (A, 128))
+        offsets.append(jnp.sum(c2, axis=0, keepdims=True))
+
+    def path_step(c, carry):
+        for b in range(width // SUB):
+            at = pl.ds(pl.multiple_of(c * width + b * SUB, SUB), SUB)
+            s, t = s_ref[:, at], t_ref[:, at]
+            up, down, flat = up_ref[:, at], down_ref[:, at], flat_ref[:, at]
+            fits, bars = [], []
+            for i in range(2):
+                square = wide(8 + 5 * i) * s
+                lead = wide(7 + 5 * i) + square + wide(9 + 5 * i) * up
+                c4 = wide(11 + 5 * i)
+                fits.append(jnp.sum(s * lead + c4 * t, axis=0, keepdims=True) - offsets[i])
+                bars.append(lead + square + wide(10 + 5 * i) * down + c4 * flat)
+            free = free_ref[:, at]
+            cont, lam = fits
+            value_ref[:, at] = rew_ref[:, at] + free * cont
+            flow_ref[:, at] = lam
+            cot_ref[:, at] = (
+                wide(5) * ((cf_ref[:, at] - cont) * bars[1] + (free - lam) * bars[0]) + wide(6) * bar_ref[:, at]
+            )
+        return carry
+
+    lax.fori_loop(0, chunks, path_step, 0)
 
     if comm:
         ag_wait(GSLOTS, SLOTS)
@@ -455,7 +494,7 @@
     glane = lax.broadcasted_iota(jnp.int32, (A, N), 1)
     both = jnp.where(glane == 0, delta, jnp.where(glane == 1, vega, 0.0)) * per_path
     both = jnp.concatenate([both, jnp.zeros((N - A, N), F32)], axis=0).T
-    greek_out[...] = both[0:8, :]
+    greek_out[...] = both[0:2, 0:A]
 
     if comm:
         def sent_slot(slot, carry):
@@ -482,88 +521,17 @@
             lax.fori_loop(1, plane, sent_ag, 0)
 
 
-def second_kernel(
-    width, s_ref, t_ref, cf_ref, free_ref, rew_ref, bar_ref, coef_ref, greek_ref, spot_hbm, vol_hbm, wei_hbm,
-    value_hbm, cot_hbm, flow_hbm, greek_hbm,
-    spot_ref, vol_ref, wei_ref, const, value_ref, cot_ref, flow_ref, greeks, par_sem, out_sem,
-):
-    local = s_ref.shape[1]
-    chunks = local // width
-    small = [
-        pltpu.make_async_copy(src, dst, par_sem.at[i])
-        for i, (src, dst) in enumerate(((spot_hbm, spot_ref), (vol_hbm, vol_ref), (wei_hbm, wei_ref)))
-    ]
-    for copy in small:
+def second_kernel(value_ref, cot_ref, flow_ref, greek_ref, value_hbm, cot_hbm, flow_hbm, greek_hbm, sem):
+    copies = [(value_ref, value_hbm), (flow_ref, flow_hbm), (greek_ref, greek_hbm)]
+    copies = [(cot_ref.at[8 * i : 8 * i + 8], cot_hbm.at[8 * i : 8 * i + 8]) for i in range(A // 8)] + copies
+    copies = [pltpu.make_async_copy(src, dst, sem.at[i]) for i, (src, dst) in enumerate(copies)]
+    for copy in copies:
         copy.start()
-
-    def outs(c):
-        at = pl.ds(pl.multiple_of(c * width, width), width)
-        return [
-            pltpu.make_async_copy(src.at[:, at], dst.at[:, at], out_sem.at[i, c])
-            for i, (src, dst) in enumerate(((cot_ref, cot_hbm), (value_ref, value_hbm), (flow_ref, flow_hbm)))
-        ]
-
-    offsets = []
-    for i in range(2):
-        c1, c2, c3, c4 = (coef_ref[A * b : A * (b + 1), i : i + 1] for b in range(4))
-        c2 = c2 * inv_root_two
-        c3d = jnp.concatenate([c3[A - 1 :], c3[: A - 1]], axis=0)
-        for j, x in enumerate((c1, c2, c3, c3d, c4)):
-            const[5 * i + j] = jnp.broadcast_to(x, (A, 128))
-        offsets.append(jnp.sum(c2, axis=0, keepdims=True))
-    greeks[...] = greek_ref[0:2, 0:A]
-    last = pltpu.make_async_copy(greeks, greek_hbm, par_sem.at[3])
-    last.start()
-    for copy in small:
+    for copy in copies:
         copy.wait()
-    vol = column(vol_ref[...], A)
-    spot = column(spot_ref[...], A)
-    weight = column(wei_ref[...], A)
-    scale = 1.0 / (spot * (vol * root_time))
-    share = weight / jnp.sum(weight * spot, axis=0, keepdims=True)
-    const[10] = jnp.broadcast_to(scale, (A, 128))
-    const[11] = jnp.broadcast_to(share, (A, 128))
-
-    def wide(i):
-        x = const[i]
-        return jnp.concatenate([x] * (SUB2 // 128), axis=1)
-
-    def step(c, carry):
-        for b in range(width // SUB2):
-            at = pl.ds(pl.multiple_of(c * width + b * SUB2, SUB2), SUB2)
-            s, t = s_ref[:, at], t_ref[:, at]
-            up, down = pltpu.roll(s, A - 1, 0), pltpu.roll(s, 1, 0)
-            flat = 1.0 - t * t
-            fits, bars = [], []
-            for i in range(2):
-                square = wide(5 * i + 1) * s
-                lead = wide(5 * i) + square + wide(5 * i + 2) * up
-                c4 = wide(5 * i + 4)
-                fits.append(jnp.sum(s * lead + c4 * t, axis=0, keepdims=True) - offsets[i])
-                bars.append(lead + square + wide(5 * i + 3) * down + c4 * flat)
-            free = free_ref[:, at]
-            cont, lam = fits
-            value_ref[:, at] = rew_ref[:, at] + free * cont
-            flow_ref[:, at] = lam
-            cot_ref[:, at] = (
-                wide(10) * ((cf_ref[:, at] - cont) * bars[1] + (free - lam) * bars[0]) + wide(11) * bar_ref[:, at]
-            )
-        for copy in outs(c):
-            copy.start()
-        return carry
-
-    lax.fori_loop(0, chunks, step, 0)
-
-    def finish(c, carry):
-        for copy in outs(c):
-            copy.wait()
-        return carry
-
-    lax.fori_loop(0, chunks, finish, 0)
-    last.wait()
-
-
-def per_device(dims, total_paths, normals, spot, vol, weights, cash_flows, exercise, width=2048, width2=2048):
+
+
+def per_device(dims, total_paths, normals, spot, vol, weights, cash_flows, exercise, width=2048):
     comm = dims is not None
     local = normals.shape[1]
     chunks = local // width
@@ -581,18 +549,16 @@
     wide, flat = jax.ShapeDtypeStruct((A, local), F32), jax.ShapeDtypeStruct((1, local), F32)
     half = pltpu.VMEM((2 * N, local // 2), BF16)
     tiny = pltpu.VMEM((1, A), F32)
-    *arrays, coef, greek = pl.pallas_call(
+    results = pl.pallas_call(
         functools.partial(first_kernel, dims, total_paths, width),
-        out_shape=(
-            wide, wide, flat, flat, flat, flat,
-            jax.ShapeDtypeStruct((N, N), F32), jax.ShapeDtypeStruct((8, N), F32),
-        ),
+        out_shape=(flat, wide, flat, jax.ShapeDtypeStruct((2, A), F32)),
         in_specs=[hbm] * 6,
-        out_specs=(vmem,) * 8,
+        out_specs=(vmem,) * 4,
         scratch_shapes=[
+            *[pltpu.VMEM((A, local), F32)] * 5, *[pltpu.VMEM((1, local), F32)] * 4,
             pltpu.VMEM((A, local), F32), tiny, tiny, tiny, pltpu.VMEM((1, local), jnp.int32),
             half, half, pltpu.VMEM((16, local), BF16), pltpu.VMEM((2, 10 * A, width), BF16),
-            pltpu.VMEM((5, A, 128), F32),
+            pltpu.VMEM((17, A, 128), F32),
             pltpu.VMEM((2 * N, 2 * N), F32), pltpu.VMEM((16, 2 * N), F32),
             pltpu.VMEM((10 * A, 2 * N), F32), pltpu.VMEM((5 * A, 128), F32),
             pltpu.VMEM((A, 128), F32), pltpu.VMEM((A, 128), F32),
@@ -607,18 +573,14 @@
         name="normal_equations",
     )(normals, spot, vol, weights, cash_flows, exercise)
     value, cot, flow, greeks = pl.pallas_call(
-        functools.partial(second_kernel, width2),
+        second_kernel,
         out_shape=(flat, wide, flat, jax.ShapeDtypeStruct((2, A), F32)),
-        in_specs=[vmem] * 8 + [hbm] * 3,
+        in_specs=[vmem] * 4,
         out_specs=(hbm,) * 4,
-        scratch_shapes=[
-            tiny, tiny, tiny, pltpu.VMEM((12, A, 128), F32),
-            pltpu.VMEM((1, local), F32), pltpu.VMEM((A, local), F32), pltpu.VMEM((1, local), F32),
-            pltpu.VMEM((2, A), F32), dma((4,)), dma((3, local // width2)),
-        ],
-        compiler_params=pltpu.CompilerParams(vmem_limit_bytes=32 * 2**20),
-        name="path_outputs",
-    )(*arrays, coef, greek, spot, vol, weights)
+        scratch_shapes=[dma((A // 8 + 3,))],
+        compiler_params=pltpu.CompilerParams(vmem_limit_bytes=4 * 2**20),
+        name="put_out",
+    )(*results)
     return value.reshape(local), cot, flow.reshape(local), greeks
 
 

time: 57.3 us -> 53.6 us (0.935)
  Pallas kernels: 56.5 us -> 52.8 us
    pallas_call x1, Pallas kernels: 5.18 us -> 1.41 us  [per_device(): pl.pallas_call(second_kernel, out_shape=(flat, wide, flat, jax.ShapeDtype...]
where the time goes in v3:
time: 53.6 us; the launch traced here: 53.5 us
  Pallas kernels  52.8 us (99%)
  between operations  0.64 us (1%)
    pallas_call x1, Pallas kernels, per_device(): pl.pallas_call(functools.partial(first_kernel, dims, total_paths, width),...  51.4 us
    pallas_call x1, Pallas kernels, per_device(): pl.pallas_call(second_kernel, out_shape=(flat, wide, flat, jax.ShapeDtype...  1.41 us

profile of v3, /device:TPU:1, one launch (start us, length us, event | category | flops | bytes accessed | tf_op | source)
XLA Modules:
  0.0 53.5 jit_solution(7382265189032744073)
XLA Ops:
  0.6 51.4 %normal_equations.1 = (f32[1,16384]{1,0:T(1,128)S(1)}, f32[32,16384]{1,0:T(8,128)S(1)}, f32[1,16384]{1,0:T(1,128)S(1)}, f32[2,32]{1,0:T(2,128)S(1)}) custom-call(f32[32,16384]{1,0:T(8,128)} %z_hbm.1, f32[1,32]{1,0:T(1,128)} %bitcast.9, f32[1,32]{1,0:T(1,128)} %bitcast.10, f32[1,32]{1,0:T(1,128)} %bitcast.11, f32[1,16384]{1,0:T(1,128)} %bitcast.7, ...), custom_call_target="tpu_custom_call" | custom-call | tf_op jit(solution)/shard_map/normal_equations/pallas_call | solution.py:552
  52.0 1.4 %put_out.1 = (f32[1,16384]{1,0:T(1,128)}, f32[32,16384]{1,0:T(8,128)}, f32[1,16384]{1,0:T(1,128)}, f32[2,32]{1,0:T(2,128)}) custom-call(f32[1,16384]{1,0:T(1,128)S(1)} %get-tuple-element.12.value_ref, f32[32,16384]{1,0:T(8,128)S(1)} %get-tuple-element.13.cot_ref, f32[1,16384]{1,0:T(1,128)S(1)} %get-tuple-element.14.flow_ref, ...), custom_call_target="tpu_custom_call" | custom-call | tf_op jit(solution)/shard_map/put_out/pallas_call | solution.py:575

commit v4 on v3

--- a/solution.py
+++ b/solution.py
@@ -36,46 +36,73 @@
     return hi, (x - hi.astype(F32)).astype(BF16)
 
 
+def pivots(tile, k, lane):
+    across = [jnp.broadcast_to(tile[:, k + j : k + j + 1], (8, N)) for j in range(4)]
+    q0 = k % 8
+
+    def at(i, j):
+        return jnp.broadcast_to(across[j][q0 + i : q0 + i + 1, :], (8, N))
+
+    a, h, c = at(0, 0), at(0, 1), at(1, 1)
+    b00, b01, b10, b11 = at(0, 2), at(0, 3), at(1, 2), at(1, 3)
+    d00, d01, d11 = at(2, 2), at(2, 3), at(3, 3)
+    inv = 1.0 / (a * c - h * h)
+    i00, i01, i11 = c * inv, -(h * inv), a * inv
+    e00, e01 = i00 * b00 + i01 * b10, i00 * b01 + i01 * b11
+    e10, e11 = i01 * b00 + i11 * b10, i01 * b01 + i11 * b11
+    s00 = d00 - (b00 * e00 + b10 * e10)
+    s01 = d01 - (b00 * e01 + b10 * e11)
+    s11 = d11 - (b01 * e01 + b11 * e11)
+    inv = 1.0 / (s00 * s11 - s01 * s01)
+    w00, w01, w11 = s11 * inv, -(s01 * inv), s00 * inv
+    r0, r1, r2, r3 = (
+        jnp.broadcast_to(tile[q0 + q : q0 + q + 1, :], (8, N)) - (lane == k + q).astype(F32) for q in range(4)
+    )
+    t2 = r2 - (e00 * r0 + e10 * r1)
+    t3 = r3 - (e01 * r0 + e11 * r1)
+    low0 = w00 * t2 + w01 * t3
+    low1 = w01 * t2 + w11 * t3
+    up0 = (i00 * r0 + i01 * r1) - (e00 * low0 + e01 * low1)
+    up1 = (i01 * r0 + i11 * r1) - (e10 * low0 + e11 * low1)
+    return across, (up0, up1, low0, low1)
+
+
+def take(x, k, w, across=None):
+    c = across or [jnp.broadcast_to(x[:, k + q : k + q + 1], (8, N)) for q in range(4)]
+    return x - ((c[0] * w[0] + c[1] * w[1]) + (c[2] * w[2] + c[3] * w[3]))
+
+
 def solve(g, b, between):
+    tiles = N // 8
     lane = lax.broadcasted_iota(jnp.int32, (8, N), 1)
-    rows = [g[8 * i : 8 * i + 8, :] for i in range(N // 8)] + [b]
-    for k in range(0, N, 4):
-        if k == N // 2:
+    sub = lax.broadcasted_iota(jnp.int32, (8, N), 0)
+    rows = [g[8 * i : 8 * i + 8, :] for i in range(tiles)] + [b]
+    for t in range(tiles):
+        if t == tiles // 2:
             between()
-        tile = rows[k // 8]
-        pivot = []
-        for q in range(4):
-            r = k % 8 + q
-            pivot.append(jnp.broadcast_to(tile[r : r + 1, :], (8, N)))
-
-        def at(i, j):
-            return jnp.broadcast_to(pivot[i][:, k + j : k + j + 1], (8, N))
-
-        a, h, c = at(0, 0), at(0, 1), at(1, 1)
-        b00, b01, b10, b11 = at(0, 2), at(0, 3), at(1, 2), at(1, 3)
-        d00, d01, d11 = at(2, 2), at(2, 3), at(3, 3)
-        inv = 1.0 / (a * c - h * h)
-        i00, i01, i11 = c * inv, -(h * inv), a * inv
-        e00, e01 = i00 * b00 + i01 * b10, i00 * b01 + i01 * b11
-        e10, e11 = i01 * b00 + i11 * b10, i01 * b01 + i11 * b11
-        s00 = d00 - (b00 * e00 + b10 * e10)
-        s01 = d01 - (b00 * e01 + b10 * e11)
-        s11 = d11 - (b01 * e01 + b11 * e11)
-        inv = 1.0 / (s00 * s11 - s01 * s01)
-        w00, w01, w11 = s11 * inv, -(s01 * inv), s00 * inv
-        r0, r1, r2, r3 = (pivot[q] - (lane == k + q).astype(F32) for q in range(4))
-        t2 = r2 - (e00 * r0 + e10 * r1)
-        t3 = r3 - (e01 * r0 + e11 * r1)
-        low0 = w00 * t2 + w01 * t3
-        low1 = w01 * t2 + w11 * t3
-        up0 = (i00 * r0 + i01 * r1) - (e00 * low0 + e01 * low1)
-        up1 = (i01 * r0 + i11 * r1) - (e10 * low0 + e11 * low1)
-        first = k // 8 if k % 8 == 0 else k // 8 + 1
-        for i in range(first, N // 8 + 1):
-            x = rows[i]
-            c0, c1, c2, c3 = (jnp.broadcast_to(x[:, k + q : k + q + 1], (8, N)) for q in range(4))
-            rows[i] = x - ((c0 * up0 + c1 * up1) + (c2 * low0 + c3 * low1))
-    return rows[N // 8]
+        k = 8 * t
+        across, first = pivots(rows[t], k, lane)
+        tile = take(rows[t], k, first, across)
+        _, second = pivots(tile, k + 4, lane)
+        rows[t + 1] = take(take(rows[t + 1], k, first), k + 4, second)
+        if t + 2 <= tiles:
+            w = jnp.where(sub < 2, jnp.where(sub < 1, first[0], first[1]), jnp.where(sub < 3, first[2], first[3]))
+            w = take(jnp.where(sub < 4, w, 0.0), k + 4, second)
+            low = jnp.where(sub < 6, jnp.where(sub < 5, second[0], second[1]), jnp.where(sub < 7, second[2], second[3]))
+            w = jnp.where(sub < 4, w, low)
+            parts = [w]
+            if t > 0:
+                parts = [jnp.zeros((k, N), F32)] + parts
+            if t + 1 < tiles:
+                parts = parts + [jnp.zeros((N - k - 8, N), F32)]
+            change = jnp.dot(
+                jnp.concatenate(rows[t + 2 :], axis=0), jnp.concatenate(parts, axis=0),
+                precision=lax.Precision.HIGHEST, preferred_element_type=F32,
+            )
+            for i in range(t + 2, tiles + 1):
+                j = 8 * (i - t - 2)
+                rows[i] = rows[i] - change[j : j + 8, :]
+    return rows[tiles]
 
 
 def first_kernel(
@@ -114,8 +141,6 @@
             pl.semaphore_signal(barrier, inc=1, device_id=peer, device_id_type=MESH)
             return carry
 
-        lax.fori_loop(1, nz, greet_z, 0)
-        lax.fori_loop(1, plane, greet_plane, 0)
 
     def in_copy(c):
         at = pl.ds(pl.multiple_of(c * width, width), width)
@@ -134,6 +159,9 @@
     small[4].start()
     for c in range(1, chunks):
         in_copy(c).start()
+    if comm:
+        lax.fori_loop(1, nz, greet_z, 0)
+        lax.fori_loop(1, plane, greet_plane, 0)
     for i in range(3):
         small[i].wait()
 
@@ -259,10 +287,10 @@
             device_id=place(me, (my_z + d) % nz), device_id_type=MESH,
         )
 
-    def ag_copy(d):
+    def ag_copy(slot):
         return pltpu.make_async_remote_copy(
-            src_ref=total.at[me], dst_ref=total.at[me], send_sem=ag_send.at[d], recv_sem=ag_recv.at[me],
-            device_id=place((me + d) % plane, my_z), device_id_type=MESH,
+            src_ref=total.at[me], dst_ref=total.at[me], send_sem=ag_send.at[slot], recv_sem=ag_recv.at[me],
+            device_id=place(slot, my_z), device_id_type=MESH,
         )
 
     def z_stage():
@@ -290,11 +318,10 @@
             parts = [parts[i] + parts[i + 1] for i in range(0, len(parts), 2)]
         total[me] = parts[0]
 
-        def send(d, carry):
-            ag_copy(d).start()
-            return carry
-
-        lax.fori_loop(1, plane, send, 0)
+        for slot in range(plane):
+            @pl.when(me != slot)
+            def _():
+                ag_copy(slot).start()
 
     def ag_wait(low, high):
         def wait(slot, carry):
@@ -514,11 +541,14 @@
 
             lax.fori_loop(1, nz, sent_z, 0)
 
-            def sent_ag(d, carry):
-                ag_copy(d).wait_send()
+            def sent_ag(slot, carry):
+                @pl.when(me != slot)
+                def _():
+                    ag_copy(slot).wait_send()
+
                 return carry
 
-            lax.fori_loop(1, plane, sent_ag, 0)
+            lax.fori_loop(0, plane, sent_ag, 0)
 
 
 def second_kernel(value_ref, cot_ref, flow_ref, greek_ref, value_hbm, cot_hbm, flow_hbm, greek_hbm, sem):

time: 53.6 us -> 52.2 us (0.974)
  Pallas kernels: 52.8 us -> 51.4 us
    pallas_call x1, Pallas kernels: 51.4 us -> 50 us  [per_device(): pl.pallas_call(functools.partial(first_kernel, dims, total_paths, width),...]
where the time goes in v4:
time: 52.2 us; the launch traced here: 52.1 us
  Pallas kernels  51.4 us (98%)
  between operations  0.64 us (1%)
    pallas_call x1, Pallas kernels, per_device(): pl.pallas_call(functools.partial(first_kernel, dims, total_paths, width),...  50 us
    pallas_call x1, Pallas kernels, per_device(): pl.pallas_call(second_kernel, out_shape=(flat, wide, flat, jax.ShapeDtype...  1.41 us

profile of v4, /device:TPU:1, one launch (start us, length us, event | category | flops | bytes accessed | tf_op | source)
XLA Modules:
  0.0 52.1 jit_solution(10691432331081722607)
XLA Ops:
  0.6 50.0 %normal_equations.1 = (f32[1,16384]{1,0:T(1,128)S(1)}, f32[32,16384]{1,0:T(8,128)S(1)}, f32[1,16384]{1,0:T(1,128)S(1)}, f32[2,32]{1,0:T(2,128)S(1)}) custom-call(f32[32,16384]{1,0:T(8,128)} %z_hbm.1, f32[1,32]{1,0:T(1,128)} %bitcast.9, f32[1,32]{1,0:T(1,128)} %bitcast.10, f32[1,32]{1,0:T(1,128)} %bitcast.11, f32[1,16384]{1,0:T(1,128)} %bitcast.7, ...), custom_call_target="tpu_custom_call" | custom-call | tf_op jit(solution)/shard_map/normal_equations/pallas_call | solution.py:582
  50.6 1.4 %put_out.1 = (f32[1,16384]{1,0:T(1,128)}, f32[32,16384]{1,0:T(8,128)}, f32[1,16384]{1,0:T(1,128)}, f32[2,32]{1,0:T(2,128)}) custom-call(f32[1,16384]{1,0:T(1,128)S(1)} %get-tuple-element.12.value_ref, f32[32,16384]{1,0:T(8,128)S(1)} %get-tuple-element.13.cot_ref, f32[1,16384]{1,0:T(1,128)S(1)} %get-tuple-element.14.flow_ref, ...), custom_call_target="tpu_custom_call" | custom-call | tf_op jit(solution)/shard_map/put_out/pallas_call | solution.py:605

commit v5 on v4

--- a/solution.py
+++ b/solution.py
@@ -20,7 +20,7 @@
 A = 32
 N = 4 * A
 GSLOTS = 9
-SUB = 256
+SUB = 512
 SLOTS = 30
 
 
@@ -352,9 +352,6 @@
             to = pl.ds(b * SUB, SUB)
             s, t = s_ref[:, at], t_ref[:, at]
             up, down, flat = pltpu.roll(s, A - 1, 0), pltpu.roll(s, 1, 0), 1.0 - t * t
-            up_ref[:, at] = up
-            down_ref[:, at] = down
-            flat_ref[:, at] = flat
             spread = wide(0)
             e = 1.0 + s * spread
             drift = e * (z_ref[:, at] - spread)
@@ -429,6 +426,18 @@
 
     if comm:
         rs_start(GSLOTS, SLOTS)
+
+    def neighbours(c, carry):
+        at = pl.ds(pl.multiple_of(c * 512, 512), 512)
+        s, t = s_ref[:, at], t_ref[:, at]
+        up_ref[:, at] = pltpu.roll(s, A - 1, 0)
+        down_ref[:, at] = pltpu.roll(s, 1, 0)
+        flat_ref[:, at] = 1.0 - t * t
+        return carry
+
+    lax.fori_loop(0, local // 512, neighbours, 0)
+
+    if comm:
 
         @pl.when(owns_rest)
         def _():

time: 52.2 us -> 52 us (level)
  no operation moved by 1% of the time
where the time goes in v5:
time: 52 us; the launch traced here: 51.9 us
  Pallas kernels  51.2 us (98%)
  between operations  0.64 us (1%)
    pallas_call x1, Pallas kernels, per_device(): pl.pallas_call(functools.partial(first_kernel, dims, total_paths, width),...  49.8 us
    pallas_call x1, Pallas kernels, per_device(): pl.pallas_call(second_kernel, out_shape=(flat, wide, flat, jax.ShapeDtype...  1.41 us

profile of v5, /device:TPU:1, one launch (start us, length us, event | category | flops | bytes accessed | tf_op | source)
XLA Modules:
  0.0 51.9 jit_solution(17560012618924920879)
XLA Ops:
  0.6 49.8 %normal_equations.1 = (f32[1,16384]{1,0:T(1,128)S(1)}, f32[32,16384]{1,0:T(8,128)S(1)}, f32[1,16384]{1,0:T(1,128)S(1)}, f32[2,32]{1,0:T(2,128)S(1)}) custom-call(f32[32,16384]{1,0:T(8,128)} %z_hbm.1, f32[1,32]{1,0:T(1,128)} %bitcast.9, f32[1,32]{1,0:T(1,128)} %bitcast.10, f32[1,32]{1,0:T(1,128)} %bitcast.11, f32[1,16384]{1,0:T(1,128)} %bitcast.7, ...), custom_call_target="tpu_custom_call" | custom-call | tf_op jit(solution)/shard_map/normal_equations/pallas_call | solution.py:591
  50.5 1.4 %put_out.1 = (f32[1,16384]{1,0:T(1,128)}, f32[32,16384]{1,0:T(8,128)}, f32[1,16384]{1,0:T(1,128)}, f32[2,32]{1,0:T(2,128)}) custom-call(f32[1,16384]{1,0:T(1,128)S(1)} %get-tuple-element.12.value_ref, f32[32,16384]{1,0:T(8,128)S(1)} %get-tuple-element.13.cot_ref, f32[1,16384]{1,0:T(1,128)S(1)} %get-tuple-element.14.flow_ref, ...), custom_call_target="tpu_custom_call" | custom-call | tf_op jit(solution)/shard_map/put_out/pallas_call | solution.py:614
